TPU v7x, 32 devices: a whole 2x2x4 slice. The times are simulated.
32 devices in a mesh: dp: 8 (over y, x, core), tensor: 4 (over z).
Axes of the slice: x: 2, y: 2, z: 4, core: 2. Of those that a mesh axis runs over, the one named last changes fastest.
Arguments:
- latent_in: bfloat16 [16, 256, 768], P('dp', 'tensor'), may hold values from -6 to 6
- condition: bfloat16 [16, 768], P('dp'), may hold values from -6 to 6
- w_ada: bfloat16 [768, 4608], P('dp', 'tensor'), may hold values from -0.21875 to 0.21875
- w_qkv: bfloat16 [3, 768, 768], P(None, 'dp', 'tensor'), may hold values from -0.21875 to 0.21875
- w_proj: bfloat16 [768, 768], P('tensor', 'dp'), may hold values from -1.25 to 1.25
- w_up: bfloat16 [768, 3072], P('dp', 'tensor'), may hold values from -0.21875 to 0.21875
- w_down: bfloat16 [3072, 768], P('tensor', 'dp'), may hold values from -0.109375 to 0.109375
- out_grad: bfloat16 [16, 256, 768], P('dp', 'tensor'), may hold values from -6 to 6
Outputs:
- latent_out: bfloat16 [16, 256, 768], P('dp', 'tensor')
- grad_latent: float32 [16, 256, 768], P('dp', 'tensor')
- grad_condition: float32 [16, 768], P('dp')
- grad_ada: float32 [768, 4608], P('dp', 'tensor')
- grad_qkv: float32 [3, 768, 768], P(None, 'dp', 'tensor')
- grad_proj: float32 [768, 768], P('tensor', 'dp')
- grad_up: float32 [768, 3072], P('dp', 'tensor')
- grad_down: float32 [3072, 768], P('tensor', 'dp')
All inputs are finite; a program needn't handle non-finite values.
Results may differ from a plain program's by a relative error of at most 0.015.
The roundings to bfloat16 on the way count: a program that leaves them out, or rounds other values in their place, can miss the bound.
Values may be sent and summed in bfloat16 or wider, within the bound.
A program may use at most 128 MiB of HBM per device.

v0:
```python
import math

import jax
import jax.numpy as jnp
from jax import lax
from jax.sharding import PartitionSpec as P

HEAD_DIM = 64
MICRO = 2


epsilon = 1e-06


def silu_value(values):
    return values / (1.0 + jnp.exp(-values))


def gelu_tanh(values):
    return (
        0.5
        * values
        * (
            1.0
            + jnp.tanh(math.sqrt(2.0 / math.pi) * (values + 0.044715 * values * values * values))
        )
    )


def normalize(values):
    centered = values - jnp.mean(values, axis=-1, keepdims=True)
    variance = jnp.mean(centered * centered, axis=-1, keepdims=True)
    return centered * lax.rsqrt(variance + epsilon)


def shards(latent_in, condition, w_ada, w_qkv, w_proj, w_up, w_down, out_grad):
    batch_rows = latent_in.shape[0] // MICRO
    head_scale = HEAD_DIM ** (-0.5)
    single_float = jnp.float32
    bf16 = jnp.bfloat16
    outs_latent = []
    outs_grad = []
    outs_cond = []
    kept_hidden = []
    kept_ffn_grad = []
    kept_ffn_in = []
    kept_pre_grad = []
    kept_mixed = []
    kept_attn_grad = []
    kept_attn_in = []
    kept_proj_grad = []
    kept_cond = []
    kept_mod_grad = []
    for micro_index in range(MICRO):
        first = micro_index * batch_rows
        last = first + batch_rows
        fwd_weights = (
            lax.all_gather(w_ada, "dp", axis=0, tiled=True),
            lax.all_gather(w_qkv, "dp", axis=1, tiled=True),
            lax.all_gather(w_proj, "dp", axis=1, tiled=True),
            lax.all_gather(w_up, "dp", axis=0, tiled=True),
            lax.all_gather(w_down, "dp", axis=1, tiled=True),
        )
        ada_full, qkv_full, proj_full, up_weight_full, down_weight_full = fwd_weights
        cond_rows = condition[first:last].astype(single_float)
        cond_act = silu_value(cond_rows).astype(bf16)
        mod_part = jnp.dot(cond_act, ada_full, preferred_element_type=single_float)
        modulation = lax.all_gather(mod_part, "tensor", axis=1, tiled=True)
        modulation = modulation.reshape(batch_rows, 6, 1, modulation.shape[1] // 6)
        shift_a = modulation[:, 0]
        scale_a = modulation[:, 1]
        gate_a = modulation[:, 2]
        shift_f = modulation[:, 3]
        scale_f = modulation[:, 4]
        gate_f = modulation[:, 5]
        tokens = latent_in[first:last].astype(single_float)
        normed_a = normalize(tokens)
        attn_in = (normed_a * (1.0 + scale_a) + shift_a).astype(bf16)
        attn_full = lax.all_gather(attn_in, "tensor", axis=1, tiled=True)
        seq_len = attn_full.shape[1]
        local_width = qkv_full.shape[2]
        local_heads = local_width // HEAD_DIM
        projected = jnp.einsum(
            "lsd,jde->jlse", attn_full, qkv_full, preferred_element_type=single_float
        ).astype(bf16)
        projected = projected.reshape(3, batch_rows, seq_len, local_heads, HEAD_DIM)
        queries = projected[0]
        key_rows = projected[1]
        value_rows = projected[2]
        scores = (
            jnp.einsum("lqhe,lkhe->lhqk", queries, key_rows, preferred_element_type=single_float)
            * head_scale
        )
        score_top = jnp.max(scores, axis=-1, keepdims=True)
        shifted = jnp.exp(scores - score_top)
        score_total = jnp.sum(shifted, axis=-1, keepdims=True)
        log_total = score_top + jnp.log(score_total)
        soft_probs = (shifted / score_total).astype(bf16)
        mixed = jnp.einsum(
            "lhqk,lkhe->lqhe", soft_probs, value_rows, preferred_element_type=single_float
        )
        mixed = mixed.reshape(batch_rows, seq_len, local_width).astype(bf16)
        attn_part = jnp.einsum("lsd,de->lse", mixed, proj_full, preferred_element_type=single_float)
        attn_out = lax.psum_scatter(attn_part, "tensor", scatter_dimension=1, tiled=True)
        resid = tokens + gate_a * attn_out
        normed_f = normalize(resid)
        ffn_in = (normed_f * (1.0 + scale_f) + shift_f).astype(bf16)
        feedforward_full = lax.all_gather(ffn_in, "tensor", axis=1, tiled=True)
        hidden_preactivation = jnp.einsum(
            "ypx,xk->ypk", feedforward_full, up_weight_full, preferred_element_type=single_float
        )
        hidden_units = gelu_tanh(hidden_preactivation).astype(bf16)
        feedforward_part = jnp.einsum(
            "jxz,zb->jxb", hidden_units, down_weight_full, preferred_element_type=single_float
        )
        ffn_out = lax.psum_scatter(
            feedforward_part.astype(jnp.bfloat16), "tensor", scatter_dimension=1, tiled=True
        ).astype(jnp.float32)
        outs_latent.append((resid + gate_f * ffn_out).astype(bf16))
        back_weights = (
            lax.all_gather(w_ada, "dp", axis=0, tiled=True),
            lax.all_gather(w_qkv, "dp", axis=1, tiled=True),
            lax.all_gather(w_proj, "dp", axis=1, tiled=True),
            lax.all_gather(w_up, "dp", axis=0, tiled=True),
            lax.all_gather(w_down, "dp", axis=1, tiled=True),
        )
        ada_back, qkv_back, proj_back, up_weight_backward, down_weight_backward = back_weights
        cotangent = out_grad[first:last].astype(single_float)
        d_gate_f = jnp.sum(cotangent * ffn_out, axis=1)
        d_ffn_out = (gate_f * cotangent).astype(bf16)
        feedforward_full_gradient = lax.all_gather(d_ffn_out, "tensor", axis=1, tiled=True)
        hidden_units_gradient = jnp.einsum(
            "upv,nv->upn",
            feedforward_full_gradient,
            down_weight_backward,
            preferred_element_type=single_float,
        )
        preactivation_gradient = jax.vjp(gelu_tanh, hidden_preactivation)[1](hidden_units_gradient)[
            0
        ].astype(bf16)
        feedforward_part_gradient = jnp.einsum(
            "hrx,nx->hrn",
            preactivation_gradient,
            up_weight_backward,
            preferred_element_type=single_float,
        )
        d_ffn_in = lax.psum_scatter(
            feedforward_part_gradient, "tensor", scatter_dimension=1, tiled=True
        )
        d_shift_f = jnp.sum(d_ffn_in, axis=1)
        d_scale_f = jnp.sum(d_ffn_in * normed_f, axis=1)
        d_resid = cotangent + jax.vjp(normalize, resid)[1](d_ffn_in * (1.0 + scale_f))[0]
        d_gate_a = jnp.sum(d_resid * attn_out, axis=1)
        d_attn_out = (gate_a * d_resid).astype(bf16)
        d_attn_full = lax.all_gather(d_attn_out, "tensor", axis=1, tiled=True)
        d_mixed = jnp.einsum(
            "lse,de->lsd", d_attn_full, proj_back, preferred_element_type=single_float
        ).astype(bf16)
        d_mixed = d_mixed.reshape(batch_rows, seq_len, local_heads, HEAD_DIM)
        again_scores = (
            jnp.einsum("lqhe,lkhe->lhqk", queries, key_rows, preferred_element_type=single_float)
            * head_scale
        )
        again_probs = jnp.exp(again_scores - log_total)
        d_probs = jnp.einsum(
            "lqhe,lkhe->lhqk", d_mixed, value_rows, preferred_element_type=single_float
        )
        d_scores = again_probs * (d_probs - jnp.sum(d_probs * again_probs, axis=-1, keepdims=True))
        d_scores = d_scores.astype(bf16)
        d_values = jnp.einsum(
            "lhqk,lqhe->lkhe",
            again_probs.astype(bf16),
            d_mixed,
            preferred_element_type=single_float,
        )
        d_queries = (
            jnp.einsum("lhqk,lkhe->lqhe", d_scores, key_rows, preferred_element_type=single_float)
            * head_scale
        )
        d_keys = (
            jnp.einsum("lhqk,lqhe->lkhe", d_scores, queries, preferred_element_type=single_float)
            * head_scale
        )
        d_projected = jnp.stack([d_queries, d_keys, d_values], axis=0)
        d_projected = d_projected.reshape(3, batch_rows, seq_len, local_width).astype(bf16)
        d_attn_part = jnp.einsum(
            "jlse,jde->lsd", d_projected, qkv_back, preferred_element_type=single_float
        )
        d_attn_in = lax.psum_scatter(
            d_attn_part.astype(jnp.bfloat16), "tensor", scatter_dimension=1, tiled=True
        ).astype(jnp.float32)
        d_shift_a = jnp.sum(d_attn_in, axis=1)
        d_scale_a = jnp.sum(d_attn_in * normed_a, axis=1)
        d_tokens = d_resid + jax.vjp(normalize, tokens)[1](d_attn_in * (1.0 + scale_a))[0]
        outs_grad.append(d_tokens)
        d_modulation = jnp.stack(
            [d_shift_a, d_scale_a, d_gate_a, d_shift_f, d_scale_f, d_gate_f], axis=1
        )
        d_modulation = d_modulation.reshape(batch_rows, 6 * d_modulation.shape[2])
        d_mod_own = lax.psum_scatter(
            d_modulation, "tensor", scatter_dimension=1, tiled=True
        ).astype(bf16)
        d_act_part = jnp.einsum(
            "le,de->ld", d_mod_own, ada_back, preferred_element_type=single_float
        )
        d_act = lax.psum(d_act_part, "tensor")
        outs_cond.append(jax.vjp(silu_value, cond_rows)[1](d_act)[0])
        kept_hidden.append(hidden_units)
        kept_ffn_grad.append(feedforward_full_gradient)
        kept_ffn_in.append(feedforward_full)
        kept_pre_grad.append(preactivation_gradient)
        kept_mixed.append(mixed)
        kept_attn_grad.append(d_attn_full)
        kept_attn_in.append(attn_full)
        kept_proj_grad.append(d_projected)
        kept_cond.append(cond_act)
        kept_mod_grad.append(d_mod_own)
    all_hidden = jnp.concatenate(kept_hidden, axis=0)
    all_ffn_grad = jnp.concatenate(kept_ffn_grad, axis=0)
    all_ffn_in = jnp.concatenate(kept_ffn_in, axis=0)
    all_pre_grad = jnp.concatenate(kept_pre_grad, axis=0)
    all_mixed = jnp.concatenate(kept_mixed, axis=0)
    all_attn_grad = jnp.concatenate(kept_attn_grad, axis=0)
    all_attn_in = jnp.concatenate(kept_attn_in, axis=0)
    all_proj_grad = jnp.concatenate(kept_proj_grad, axis=1)
    all_cond = jnp.concatenate(kept_cond, axis=0)
    all_mod_grad = jnp.concatenate(kept_mod_grad, axis=0)
    grad_down = jnp.einsum(
        "wvx,wvu->xu", all_hidden, all_ffn_grad, preferred_element_type=single_float
    )
    grad_up = jnp.einsum(
        "wzy,wzo->yo", all_ffn_in, all_pre_grad, preferred_element_type=single_float
    )
    grad_proj = jnp.einsum(
        "lsd,lse->de", all_mixed, all_attn_grad, preferred_element_type=single_float
    )
    grad_qkv = jnp.einsum(
        "lsd,jlse->jde", all_attn_in, all_proj_grad, preferred_element_type=single_float
    )
    grad_ada = jnp.einsum("ld,le->de", all_cond, all_mod_grad, preferred_element_type=single_float)
    shard_grads = (
        lax.psum_scatter(grad_ada, "dp", scatter_dimension=0, tiled=True),
        lax.psum_scatter(grad_qkv, "dp", scatter_dimension=1, tiled=True),
        lax.psum_scatter(grad_proj, "dp", scatter_dimension=1, tiled=True),
        lax.psum_scatter(grad_up, "dp", scatter_dimension=0, tiled=True),
        lax.psum_scatter(grad_down, "dp", scatter_dimension=1, tiled=True),
    )
    latent_out = jnp.concatenate(outs_latent, axis=0)
    grad_latent = jnp.concatenate(outs_grad, axis=0)
    grad_condition = jnp.concatenate(outs_cond, axis=0)
    return (
        latent_out,
        grad_latent,
        grad_condition,
        shard_grads[0],
        shard_grads[1],
        shard_grads[2],
        shard_grads[3],
        shard_grads[4],
    )


def solution(mesh):
    return jax.shard_map(
        shards,
        mesh=mesh,
        in_specs=(
            P("dp", "tensor", None),
            P("dp", None),
            P("dp", "tensor"),
            P(None, "dp", "tensor"),
            P("tensor", "dp"),
            P("dp", "tensor"),
            P("tensor", "dp"),
            P("dp", "tensor", None),
        ),
        out_specs=(
            P("dp", "tensor", None),
            P("dp", "tensor", None),
            P("dp", None),
            P("dp", "tensor"),
            P(None, "dp", "tensor"),
            P("tensor", "dp"),
            P("dp", "tensor"),
            P("tensor", "dp"),
        ),
        check_vma=False,
    )
```

profile of v0, /device:TPU:0, one launch (start us, length us, event | category | flops | bytes accessed | tf_op | source)
XLA Modules:
  0.0 736.4 jit_solution(68364564783903809)
XLA Ops:
  9.9 17.9 %all_gather.63 = bf16[3,768,192]{2,0,1:T(4,128)(2,1)} all-gather(bf16[3,96,192]{2,0,1:T(4,128)(2,1)S(1)} %copy.44), channel_id=1, replica_groups=mesh['dp'=8,'tensor'=4] {'dp'}, dimensions={1}, use_global_device_ids=true | all-gather | bytes 995328 | tf_op jit(solution)/shard_map/all_gather | solution.py:59
  43.8 13.2 %all-gather.2 = f32[4,1,1152]{2,1,0:T(1,128)S(1)} all-gather(f32[1,1,1152]{2,1,0:T(1,128)S(1)} %convolution_bitcast_fusion.1), channel_id=2, replica_groups=mesh['dp'=8,'tensor'=4] {'tensor'}, dimensions={0}, use_global_device_ids=true | all-gather | bytes 23040 | tf_op jit(solution)/shard_map/all_gather | solution.py:68
  57.3 15.3 %all_gather.62 = bf16[1,256,768]{2,1,0:T(8,128)(2,1)S(1)} all-gather(bf16[1,64,768]{2,1,0:T(8,128)(2,1)S(1)} %fusion.101), channel_id=1, replica_groups=mesh['dp'=8,'tensor'=4] {'tensor'}, dimensions={1}, use_global_device_ids=true | all-gather | bytes 491520 | tf_op jit(solution)/shard_map/all_gather | solution.py:79
  76.8 18.0 %all_gather.71 = bf16[1,256,768]{2,1,0:T(8,128)(2,1)} all-gather(bf16[1,64,768]{2,1,0:T(8,128)(2,1)S(1)} %fusion.110), channel_id=1, replica_groups=mesh['dp'=8,'tensor'=4] {'tensor'}, dimensions={1}, use_global_device_ids=true | all-gather | bytes 491520 | tf_op jit(solution)/shard_map/all_gather | solution.py:131
  101.7 14.3 %all_gather.65 = bf16[1,256,768]{2,1,0:T(8,128)(2,1)S(1)} all-gather(bf16[1,64,768]{2,1,0:T(8,128)(2,1)S(1)} %add_convert_fusion.1), channel_id=1, replica_groups=mesh['dp'=8,'tensor'=4] {'tensor'}, dimensions={1}, use_global_device_ids=true | all-gather | bytes 491520 | tf_op jit(solution)/shard_map/all_gather | solution.py:108
  128.2 23.2 %all-gather.12.cloned.1.call-done = bf16[768,768]{0,1:T(8,128)(2,1)} async-done(((bf16[768,96]{0,1:T(8,128)(2,1)}), bf16[768,768]{0,1:T(8,128)(2,1)}) %all-gather.12.cloned.1.call-update) | async-done | bytes 1179664 | tf_op jit(solution)/shard_map/all_gather | solution.py:62
  158.8 13.5 %all-gather.3 = f32[4,1,1152]{2,1,0:T(1,128)S(1)} all-gather(f32[1,1,1152]{2,1,0:T(1,128)S(1)} %convolution_bitcast_fusion), channel_id=3, replica_groups=mesh['dp'=8,'tensor'=4] {'tensor'}, dimensions={0}, use_global_device_ids=true | all-gather | bytes 23040 | tf_op jit(solution)/shard_map/all_gather | solution.py:68
  181.1 20.4 %reduce-scatter.26.cloned.1.call-done = bf16[1,64,768]{2,1,0:T(8,128)(2,1)} async-done(((bf16[1,256,768]{2,1,0:T(8,128)(2,1)}), bf16[1,64,768]{2,1,0:T(8,128)(2,1)}) %reduce-scatter.26.cloned.1.call-update) | async-done | bytes 98320 | tf_op jit(solution)/shard_map/reduce_scatter | solution.py:116
  204.9 14.8 %all_gather.72 = bf16[1,256,768]{2,1,0:T(8,128)(2,1)S(1)} all-gather(bf16[1,64,768]{2,1,0:T(8,128)(2,1)S(1)} %get-tuple-element.84), channel_id=1, replica_groups=mesh['dp'=8,'tensor'=4] {'tensor'}, dimensions={1}, use_global_device_ids=true | all-gather | bytes 491520 | tf_op jit(solution)/shard_map/all_gather | solution.py:155
  223.6 18.8 %reduce-scatter.34.cloned.1.call-done = bf16[1,64,768]{2,1,0:T(8,128)(2,1)} async-done(((bf16[1,256,768]{2,1,0:T(8,128)(2,1)}), bf16[1,64,768]{2,1,0:T(8,128)(2,1)}) %reduce-scatter.34.cloned.1.call-update) | async-done | bytes 98320 | tf_op jit(solution)/shard_map/reduce_scatter | solution.py:189
  246.7 14.6 %all_gather.69 = bf16[1,256,768]{2,1,0:T(8,128)(2,1)S(1)} all-gather(bf16[1,64,768]{2,1,0:T(8,128)(2,1)S(1)} %fusion.99), channel_id=1, replica_groups=mesh['dp'=8,'tensor'=4] {'tensor'}, dimensions={1}, use_global_device_ids=true | all-gather | bytes 491520 | tf_op jit(solution)/shard_map/all_gather | solution.py:79
  264.7 17.6 %all_gather.73 = bf16[1,256,768]{2,1,0:T(8,128)(2,1)} all-gather(bf16[1,64,768]{2,1,0:T(8,128)(2,1)S(1)} %copy-done.52), channel_id=1, replica_groups=mesh['dp'=8,'tensor'=4] {'tensor'}, dimensions={1}, use_global_device_ids=true | all-gather | bytes 491520 | tf_op jit(solution)/shard_map/all_gather | solution.py:131
  290.6 15.1 %all_gather.70 = bf16[1,256,768]{2,1,0:T(8,128)(2,1)S(1)} all-gather(bf16[1,64,768]{2,1,0:T(8,128)(2,1)S(1)} %add_convert_fusion), channel_id=1, replica_groups=mesh['dp'=8,'tensor'=4] {'tensor'}, dimensions={1}, use_global_device_ids=true | all-gather | bytes 491520 | tf_op jit(solution)/shard_map/all_gather | solution.py:108
  315.4 18.1 %reduce-scatter.36.cloned.1.call-done = f32[1,64,768]{2,1,0:T(8,128)} async-done(((f32[1,256,768]{2,1,0:T(8,128)}), f32[1,64,768]{2,1,0:T(8,128)}) %reduce-scatter.36.cloned.1.call-update) | async-done | bytes 196624 | tf_op jit(solution)/shard_map/reduce_scatter | solution.py:147
  336.3 19.8 %reduce-scatter.30.cloned.1.call-done = bf16[1,64,768]{2,1,0:T(8,128)(2,1)} async-done(((bf16[1,256,768]{2,1,0:T(8,128)(2,1)}), bf16[1,64,768]{2,1,0:T(8,128)(2,1)}) %reduce-scatter.30.cloned.1.call-update) | async-done | bytes 98320 | tf_op jit(solution)/shard_map/reduce_scatter | solution.py:116
  359.8 14.8 %all_gather.74 = bf16[1,256,768]{2,1,0:T(8,128)(2,1)S(1)} all-gather(bf16[1,64,768]{2,1,0:T(8,128)(2,1)S(1)} %get-tuple-element.81), channel_id=1, replica_groups=mesh['dp'=8,'tensor'=4] {'tensor'}, dimensions={1}, use_global_device_ids=true | all-gather | bytes 491520 | tf_op jit(solution)/shard_map/all_gather | solution.py:155
  378.9 18.6 %reduce-scatter.38.cloned.1.call-done = bf16[1,64,768]{2,1,0:T(8,128)(2,1)} async-done(((bf16[1,256,768]{2,1,0:T(8,128)(2,1)}), bf16[1,64,768]{2,1,0:T(8,128)(2,1)}) %reduce-scatter.38.cloned.1.call-update) | async-done | bytes 98320 | tf_op jit(solution)/shard_map/reduce_scatter | solution.py:189
  436.2 17.0 %reduce-scatter.46.cloned.1.call-done = f32[1152,1]{1,0:T(8,128)} async-done(((f32[4608,1]{1,0:T(8,128)}), f32[1152,1]{1,0:T(8,128)}) %reduce-scatter.46.cloned.1.call-update) | async-done | bytes 4624
  454.4 48.6 %reduce-scatter.48.cloned.1.call-done = f32[1152,1]{1,0:T(8,128)} async-done(((f32[4608,1]{1,0:T(8,128)}), f32[1152,1]{1,0:T(8,128)}) %reduce-scatter.48.cloned.1.call-update) | async-done | bytes 4624
  521.2 19.4 %reduce-scatter.52.cloned.1.call-done = f32[96,192]{1,0:T(8,128)} async-done(((f32[768,192]{1,0:T(8,128)}), f32[96,192]{1,0:T(8,128)}) %reduce-scatter.52.cloned.1.call-update) | async-done | bytes 73744
  542.2 42.0 %reduce-scatter.50.cloned.1.call-done = f32[96,576]{1,0:T(8,128)} async-done(((f32[768,576]{1,0:T(8,128)}), f32[96,576]{1,0:T(8,128)}) %reduce-scatter.50.cloned.1.call-update) | async-done | bytes 221200
  586.1 44.7 %reduce-scatter.42.cloned.1.call-done = f32[96,768]{1,0:T(8,128)} async-done(((f32[768,768]{1,0:T(8,128)}), f32[96,768]{1,0:T(8,128)}) %reduce-scatter.42.cloned.1.call-update) | async-done | bytes 294928 | tf_op jit(solution)/shard_map/reduce_scatter | solution.py:245
  630.8 46.3 %reduce-scatter.44.cloned.1.call-done = f32[768,96]{0,1:T(8,128)} async-done(((f32[768,768]{0,1:T(8,128)}), f32[768,96]{0,1:T(8,128)}) %reduce-scatter.44.cloned.1.call-update) | async-done | bytes 294928 | tf_op jit(solution)/shard_map/reduce_scatter | solution.py:246
  677.1 52.4 %reduce-scatter.40.cloned.1.call-done = f32[96,1152]{1,0:T(8,128)} async-done(((f32[768,1152]{1,0:T(8,128)}), f32[96,1152]{1,0:T(8,128)}) %reduce-scatter.40.cloned.1.call-update) | async-done | bytes 442384 | tf_op jit(solution)/shard_map/reduce_scatter | solution.py:242
  (363 shorter events, 162.2 us)
Async XLA Ops:
  7.2 34.8 %all-gather.8.cloned.1.call-start = ((), (), s32[]{:S(2)}) async-start(), calls=%async_computation.15 | async-start | bytes 1990656 | tf_op jit(solution)/shard_map/all_gather | solution.py:58
  7.9 92.4 %reduce-scatter.24.cloned.1.call-start = ((), (), s32[]{:S(2)}) async-start(), calls=%async_computation.16 | async-start | bytes 983040 | tf_op jit(solution)/shard_map/reduce_scatter | solution.py:104
  30.4 42.7 %copy-start.4 = (bf16[3,768,192]{1,2,0:T(8,128)(2,1)}, bf16[3,768,192]{1,2,0:T(8,128)(2,1)S(1)}, u32[]{:S(2)}) copy-start(bf16[3,768,192]{1,2,0:T(8,128)(2,1)S(1)} %copy.45) | copy-start | bytes 2654212
  57.2 43.1 %copy-start.66 = (f32[768]{0:T(1024)}, f32[768]{0:T(1024)S(1)}, u32[]{:S(2)}) copy-start(f32[768]{0:T(1024)S(1)} %get-tuple-element.56) | copy-start | bytes 9220
  57.2 121.7 %copy-start.61 = (f32[768]{0:T(1024)}, f32[768]{0:T(1024)S(1)}, u32[]{:S(2)}) copy-start(f32[768]{0:T(1024)S(1)} %get-tuple-element.53) | copy-start | bytes 9220
  75.4 50.2 %all-gather.10.cloned.1.call-start = ((), (), s32[]{:S(2)}) async-start(), calls=%async_computation.17 | async-start | bytes 1327104 | tf_op jit(solution)/shard_map/all_gather | solution.py:61
  76.1 75.3 %all-gather.12.cloned.1.call-start = ((), (), s32[]{:S(2)}) async-start(), calls=%async_computation.18 | async-start | bytes 1327104 | tf_op jit(solution)/shard_map/all_gather | solution.py:62
  76.7 102.2 %reduce-scatter.32.cloned.1.call-start = ((), (), s32[]{:S(2)}) async-start(), calls=%async_computation.22 | async-start | bytes 983040 | tf_op jit(solution)/shard_map/reduce_scatter | solution.py:147
  101.4 77.5 %copy-start.79 = (f32[64]{0:T(128)}, f32[64]{0:T(128)S(1)}, u32[]{:S(2)}) copy-start(f32[64]{0:T(128)S(1)} %broadcast_multiply_fusion.2) | copy-start | bytes 772
  101.6 77.3 %copy-start.87 = (f32[64]{0:T(128)}, f32[64]{0:T(128)S(1)}, u32[]{:S(2)}) copy-start(f32[64]{0:T(128)S(1)} %fusion.143) | copy-start | bytes 772
  155.3 46.2 %reduce-scatter.26.cloned.1.call-start = ((), (), s32[]{:S(2)}) async-start(), calls=%async_computation.19 | async-start | bytes 491520 | tf_op jit(solution)/shard_map/reduce_scatter | solution.py:116
  158.4 84.0 %reduce-scatter.34.cloned.1.call-start = ((), (), s32[]{:S(2)}) async-start(), calls=%async_computation.23 | async-start | bytes 491520 | tf_op jit(solution)/shard_map/reduce_scatter | solution.py:189
  222.2 39.1 %copy-start.6 = (bf16[3,768,192]{1,2,0:T(8,128)(2,1)S(1)}, bf16[3,768,192]{1,2,0:T(8,128)(2,1)}, u32[]{:S(2)}) copy-start(bf16[3,768,192]{1,2,0:T(8,128)(2,1)} %copy-done.4) | copy-start | bytes 2654212
  223.5 64.8 %reduce-scatter.28.cloned.1.call-start = ((), (), s32[]{:S(2)}) async-start(), calls=%async_computation.20 | async-start | bytes 983040 | tf_op jit(solution)/shard_map/reduce_scatter | solution.py:104
  264.7 68.8 %reduce-scatter.36.cloned.1.call-start = ((), (), s32[]{:S(2)}) async-start(), calls=%async_computation.24 | async-start | bytes 983040 | tf_op jit(solution)/shard_map/reduce_scatter | solution.py:147
  311.1 44.9 %reduce-scatter.30.cloned.1.call-start = ((), (), s32[]{:S(2)}) async-start(), calls=%async_computation.21 | async-start | bytes 491520 | tf_op jit(solution)/shard_map/reduce_scatter | solution.py:116
  314.0 83.4 %reduce-scatter.38.cloned.1.call-start = ((), (), s32[]{:S(2)}) async-start(), calls=%async_computation.25 | async-start | bytes 491520 | tf_op jit(solution)/shard_map/reduce_scatter | solution.py:189
  378.7 74.5 %reduce-scatter.46.cloned.1.call-start = ((), (), s32[]{:S(2)}) async-start(), calls=%async_computation.29 | async-start | bytes 2949120
  406.7 96.4 %reduce-scatter.48.cloned.1.call-start = ((), (), s32[]{:S(2)}) async-start(), calls=%async_computation.30 | async-start | bytes 2949120
  412.1 128.5 %reduce-scatter.52.cloned.1.call-start = ((), (), s32[]{:S(2)}) async-start(), calls=%async_computation.32 | async-start | bytes 884736
  415.5 168.7 %reduce-scatter.50.cloned.1.call-start = ((), (), s32[]{:S(2)}) async-start(), calls=%async_computation.31 | async-start | bytes 2211840
  427.5 203.3 %reduce-scatter.42.cloned.1.call-start = ((), (), s32[]{:S(2)}) async-start(), calls=%async_computation.27 | async-start | bytes 2654208 | tf_op jit(solution)/shard_map/reduce_scatter | solution.py:245
  431.1 246.0 %reduce-scatter.44.cloned.1.call-start = ((), (), s32[]{:S(2)}) async-start(), calls=%async_computation.28 | async-start | bytes 2654208 | tf_op jit(solution)/shard_map/reduce_scatter | solution.py:246
  436.1 293.4 %reduce-scatter.40.cloned.1.call-start = ((), (), s32[]{:S(2)}) async-start(), calls=%async_computation.26 | async-start | bytes 3981312 | tf_op jit(solution)/shard_map/reduce_scatter | solution.py:242
  (91 other events, 811.8 us)
Sparse Core Ops, SparseCore 0:
  9.9 32.0 all-gather.7
  75.5 24.7 reduce-scatter.23
  102.2 23.2 all-gather.9
  127.3 24.0 all-gather.11
  155.4 23.3 reduce-scatter.31
  181.6 19.8 reduce-scatter.25
  223.6 18.6 reduce-scatter.33
  264.8 23.4 reduce-scatter.27
  311.2 22.2 reduce-scatter.35
  336.2 19.7 reduce-scatter.29
  378.8 18.6 reduce-scatter.37
  406.8 46.3 reduce-scatter.45
  455.5 47.5 reduce-scatter.47
  506.0 34.5 reduce-scatter.51
  543.8 40.3 reduce-scatter.49
  588.3 42.4 reduce-scatter.41
  634.6 42.4 reduce-scatter.43
  681.4 48.0 reduce-scatter.39
where the time goes:
time: 738 us; the launch traced here: 736 us
  waiting for transfers between devices  419 us (57%)
  blocking collectives  189 us (26%)
  matrix products  40.5 us (5%)
  local copies, waits for them, and re-layouts  40.3 us (5%)
  other arithmetic  30.3 us (4%)
  between operations  15.7 us (2%)
    unnamed x22, waiting for transfers between devices  129 us
    reduce_scatter x1, waiting for transfers between devices, shards(): lax.psum_scatter(grad_ada, 'dp', scatter_dimension=0, tiled=True)  52.4 us
    reduce_scatter x1, waiting for transfers between devices, shards(): lax.psum_scatter(grad_down, 'dp', scatter_dimension=1, tiled=True)  46.3 us
    reduce_scatter x1, waiting for transfers between devices, shards(): lax.psum_scatter(grad_up, 'dp', scatter_dimension=0, tiled=True)  44.7 us
    reduce_scatter x2, waiting for transfers between devices, shards(): lax.psum_scatter(feedforward_part.astype(jnp.bfloat16), 'tensor', scatter...  40.1 us
    unnamed x209, local copies, waits for them, and re-layouts  37.5 us
    reduce_scatter x2, waiting for transfers between devices, shards(): lax.psum_scatter(d_attn_part.astype(jnp.bfloat16), 'tensor', scatter_dime...  37.4 us
    all_gather x2, blocking collectives, shards(): lax.all_gather(d_ffn_out, 'tensor', axis=1, tiled=True)  35.6 us
  transfers between devices with their start and end apart: 18, of which 18 were waited for; matrix products, arithmetic and copies ran while one was open for 8% of the time, Pallas kernels for 0%

commit v1 on v0

v1 whole, which is shorter than its diff:
```python
import math

import jax
import jax.numpy as jnp
from jax import lax
from jax.sharding import PartitionSpec as P

HEAD_DIM = 64
EPS = 1e-06
f32 = jnp.float32
bf16 = jnp.bfloat16


def silu_value(values):
    return values / (1.0 + jnp.exp(-values))


def gelu_tanh(values):
    return (
        0.5
        * values
        * (
            1.0
            + jnp.tanh(math.sqrt(2.0 / math.pi) * (values + 0.044715 * values * values * values))
        )
    )


def norm_parts(values):
    centered = values - jnp.mean(values, axis=-1, keepdims=True)
    variance = jnp.mean(centered * centered, axis=-1, keepdims=True)
    inverse = lax.rsqrt(variance + EPS)
    return centered * inverse, inverse


def norm_back(normed, inverse, grad):
    return inverse * (
        grad
        - jnp.mean(grad, axis=-1, keepdims=True)
        - normed * jnp.mean(grad * normed, axis=-1, keepdims=True)
    )


def dot(form, left, right):
    return jnp.einsum(form, left, right, preferred_element_type=f32)


def gather_tensor(block, axis):
    return lax.all_gather(block, "tensor", axis=axis, tiled=True)


def reduce_tensor(part):
    return lax.psum(part.astype(bf16), "tensor").astype(f32)


def scatter_tensor(part):
    return lax.psum_scatter(
        part.astype(bf16), "tensor", scatter_dimension=1, tiled=True
    ).astype(f32)


def gather_weights(shard):
    return lax.all_gather(shard, "dp", axis=0, tiled=True)


def scatter_grads(grads):
    return lax.psum_scatter(grads.astype(bf16), "dp", scatter_dimension=0, tiled=True).astype(f32)


def modulation_of(cond_mine, w_ada):
    part = jnp.dot(cond_mine, w_ada, preferred_element_type=f32)
    own = lax.psum_scatter(part, "dp", scatter_dimension=0, tiled=True)
    return lax.all_gather(own, "tensor", axis=1, tiled=True)


def shards(latent_in, condition, w_ada, w_qkv, w_proj, w_up, w_down, out_grad):
    rows, own_tokens, width = latent_in.shape
    scale = HEAD_DIM ** (-0.5)
    dp_at = lax.axis_index("dp")
    tensor_at = lax.axis_index("tensor")
    shard_rows = w_ada.shape[0]
    local = w_proj.shape[0]
    heads = local // HEAD_DIM
    units = w_down.shape[0]

    attn_shard = jnp.concatenate(
        [w_qkv[0], w_qkv[1], w_qkv[2], w_proj.T], axis=1
    )
    ffn_shard = jnp.concatenate([w_up, w_down.T], axis=1)
    cond_all = lax.all_gather(condition, "dp", axis=0, tiled=True)
    cond_act = silu_value(cond_all.astype(f32)).astype(bf16)
    cond_mine = lax.dynamic_slice_in_dim(cond_act, dp_at * shard_rows, shard_rows, 1)
    modulation = modulation_of(cond_mine, w_ada).reshape(rows, 6, 1, width)
    shift_a, scale_a, gate_a, shift_f, scale_f, gate_f = (modulation[:, i] for i in range(6))

    attn_weights = gather_weights(attn_shard)
    w_in = attn_weights[:, : 3 * local]
    proj_t = attn_weights[:, 3 * local :]
    both = gather_tensor(jnp.stack([latent_in, out_grad], axis=0), 2)
    ffn_weights = gather_weights(ffn_shard)
    up = ffn_weights[:, :units]
    down_t = ffn_weights[:, units:]

    tokens = both[0].astype(f32)
    cotangent = both[1].astype(f32)
    seq = tokens.shape[1]

    normed_a, inverse_a = norm_parts(tokens)
    attn_in = (normed_a * (1.0 + scale_a) + shift_a).astype(bf16)
    projected = dot("lsd,de->lse", attn_in, w_in).astype(bf16)
    projected = projected.reshape(rows, seq, 3, heads, HEAD_DIM)
    queries, keys, values = projected[:, :, 0], projected[:, :, 1], projected[:, :, 2]
    scores = dot("lqhe,lkhe->lhqk", queries, keys) * scale
    shifted = jnp.exp(scores - jnp.max(scores, axis=-1, keepdims=True))
    probs = shifted / jnp.sum(shifted, axis=-1, keepdims=True)
    probs_low = probs.astype(bf16)
    mixed = dot("lhqk,lkhe->lqhe", probs_low, values).reshape(rows, seq, local).astype(bf16)
    attn_out = reduce_tensor(dot("lsd,ed->lse", mixed, proj_t))
    resid = tokens + gate_a * attn_out
    normed_f, inverse_f = norm_parts(resid)
    ffn_in = (normed_f * (1.0 + scale_f) + shift_f).astype(bf16)
    hidden_pre = dot("lsd,dn->lsn", ffn_in, up)
    hidden, gelu_pull = jax.vjp(gelu_tanh, hidden_pre)
    hidden = hidden.astype(bf16)
    d_ffn_out = (gate_f * cotangent).astype(bf16)
    d_hidden_pre = gelu_pull(dot("lse,en->lsn", d_ffn_out, down_t))[0].astype(bf16)
    d_ffn_in = reduce_tensor(dot("lsn,dn->lsd", d_hidden_pre, up))

    ffn_part = dot("lsn,en->lse", hidden, down_t)
    d_gate_f = jnp.sum(cotangent * ffn_part, axis=1)
    ffn_own = scatter_tensor(ffn_part)
    first = tensor_at * own_tokens
    resid_own = lax.dynamic_slice_in_dim(resid, first, own_tokens, 1)
    latent_out = (resid_own + gate_f * ffn_own).astype(bf16)

    grad_ffn = jnp.concatenate(
        [dot("lsd,lsn->dn", ffn_in, d_hidden_pre), dot("lse,lsn->en", d_ffn_out, hidden)], axis=1
    )
    grad_ffn = scatter_grads(grad_ffn)

    d_shift_f = jnp.sum(d_ffn_in, axis=1)
    d_scale_f = jnp.sum(d_ffn_in * normed_f, axis=1)
    d_resid = cotangent + norm_back(normed_f, inverse_f, d_ffn_in * (1.0 + scale_f))
    d_gate_a = jnp.sum(d_resid * attn_out, axis=1)
    d_attn_out = (gate_a * d_resid).astype(bf16)
    d_mixed = dot("lse,ed->lsd", d_attn_out, proj_t).astype(bf16)
    d_mixed = d_mixed.reshape(rows, seq, heads, HEAD_DIM)
    d_probs = dot("lqhe,lkhe->lhqk", d_mixed, values)
    d_scores = probs * (d_probs - jnp.sum(d_probs * probs, axis=-1, keepdims=True))
    d_scores = d_scores.astype(bf16)
    d_values = dot("lhqk,lqhe->lkhe", probs_low, d_mixed)
    d_queries = dot("lhqk,lkhe->lqhe", d_scores, keys) * scale
    d_keys = dot("lhqk,lqhe->lkhe", d_scores, queries) * scale
    d_projected = jnp.stack([d_queries, d_keys, d_values], axis=2)
    d_projected = d_projected.reshape(rows, seq, 3 * local).astype(bf16)
    d_attn_part = dot("lse,de->lsd", d_projected, w_in)

    d_attn_own = scatter_tensor(d_attn_part)
    grad_attn = jnp.concatenate(
        [dot("lsd,lse->de", attn_in, d_projected), dot("lse,lsd->ed", d_attn_out, mixed)], axis=1
    )
    grad_attn = scatter_grads(grad_attn)

    own = lambda value: lax.dynamic_slice_in_dim(value, first, own_tokens, 1)
    grad_latent = own(d_resid) + norm_back(
        own(normed_a), own(inverse_a), d_attn_own * (1.0 + scale_a)
    )

    d_shift_a = jnp.sum(d_attn_part, axis=1)
    d_scale_a = jnp.sum(d_attn_part * normed_a, axis=1)
    ones = jnp.where(tensor_at == 0, 1.0, 0.0)
    d_modulation = jnp.concatenate(
        [d_shift_a, d_scale_a, d_gate_a * ones, d_shift_f * ones, d_scale_f * ones, d_gate_f],
        axis=1,
    )
    d_mod_own = lax.psum_scatter(d_modulation, "tensor", scatter_dimension=1, tiled=True)
    d_mod_all = lax.all_gather(d_mod_own.astype(bf16), "dp", axis=0, tiled=True)
    grad_ada = dot("ld,le->de", cond_mine, d_mod_all)
    act_part = dot("le,de->ld", d_mod_all, w_ada)
    act_all = lax.all_gather(act_part, ("dp", "tensor"), axis=0, tiled=False)
    act_all = act_all.reshape(-1, lax.axis_size("tensor"), cond_all.shape[0], shard_rows)
    act_own = lax.dynamic_slice_in_dim(act_all, dp_at * rows, rows, 2)
    d_act = jnp.sum(act_own, axis=1).transpose(1, 0, 2).reshape(rows, width)
    grad_condition = jax.vjp(silu_value, condition.astype(f32))[1](d_act)[0]

    grad_qkv = jnp.stack([grad_attn[:, j * local : (j + 1) * local] for j in range(3)], axis=0)
    grad_proj = grad_attn[:, 3 * local :].T
    grad_up = grad_ffn[:, :units]
    grad_down = grad_ffn[:, units:].T
    return (
        latent_out,
        grad_latent,
        grad_condition,
        grad_ada,
        grad_qkv,
        grad_proj,
        grad_up,
        grad_down,
    )


def solution(mesh):
    return jax.shard_map(
        shards,
        mesh=mesh,
        in_specs=(
            P("dp", "tensor", None),
            P("dp", None),
            P("dp", "tensor"),
            P(None, "dp", "tensor"),
            P("tensor", "dp"),
            P("dp", "tensor"),
            P("tensor", "dp"),
            P("dp", "tensor", None),
        ),
        out_specs=(
            P("dp", "tensor", None),
            P("dp", "tensor", None),
            P("dp", None),
            P("dp", "tensor"),
            P(None, "dp", "tensor"),
            P("tensor", "dp"),
            P("dp", "tensor"),
            P("tensor", "dp"),
        ),
        check_vma=False,
    )
```

time: 738 us -> 404 us (0.55)
  waiting for transfers between devices: 419 us -> 209 us
  blocking collectives: 189 us -> 102 us
  local copies, waits for them, and re-layouts: 40.3 us -> 23 us
  matrix products: 40.5 us -> 28.9 us
  other arithmetic: 30.3 us -> 21.2 us
    reduce_scatter x11 -> x2, waiting for transfers between devices: 256 us -> 0.03 us  [scatter_tensor(): lax.psum_scatter(part.astype(bf16), 'tensor', scatter_dimension=1, tiled=...]
    psum x0 -> x2, waiting for transfers between devices: none -> 86.7 us  [reduce_tensor(): return lax.psum(part.astype(bf16), 'tensor').astype(f32)]
    all_gather x12 -> x4, blocking collectives: 179 us -> 102 us  [the longest x1 69.4 us: shards(): act_all = lax.all_gather(act_part, ('dp', 'tensor'), axis=0, tiled=False)]
    all_gather x3, waiting for transfers between devices: 33.8 us -> 0.07 us  [the longest x2 0.05 us: gather_weights(): return lax.all_gather(shard, 'dp', axis=0, tiled=True)]
    unnamed x209 -> x86, local copies, waits for them, and re-layouts: 37.5 us -> 22 us
    dot_general x35 -> x20, matrix products: 39.6 us -> 27.2 us  [the longest x19 26.4 us: dot(): return jnp.einsum(form, left, right, preferred_element_type=f32)]
    psum x1 -> x0, blocking collectives: 10.1 us -> none  [shards(): d_act = lax.psum(d_act_part, 'tensor')]
    unnamed x22 -> x15, waiting for transfers between devices: 129 us -> 123 us
  transfers between devices with their start and end apart: 18 -> 11, of which waited for: 18 -> 6; matrix products, arithmetic and copies ran while one was open for 8% -> 9% of each run, Pallas kernels for 0% -> 0%
where the time goes in v1:
time: 404 us; the launch traced here: 403 us
  waiting for transfers between devices  209 us (52%)
  blocking collectives  102 us (25%)
  matrix products  28.9 us (7%)
  local copies, waits for them, and re-layouts  23 us (6%)
  other arithmetic  21.2 us (5%)
  between operations  17.1 us (4%)
    unnamed x15, waiting for transfers between devices  123 us
    psum x2, waiting for transfers between devices, reduce_tensor(): return lax.psum(part.astype(bf16), 'tensor').astype(f32)  86.7 us
    all_gather x1, blocking collectives, shards(): act_all = lax.all_gather(act_part, ('dp', 'tensor'), axis=0, tiled=False)  69.4 us
    dot_general x19, matrix products, dot(): return jnp.einsum(form, left, right, preferred_element_type=f32)  26.4 us
    unnamed x86, local copies, waits for them, and re-layouts  22 us
    all_gather x1, blocking collectives, modulation_of(): return lax.all_gather(own, 'tensor', axis=1, tiled=True)  13.2 us
    all_gather x1, blocking collectives, shards(): cond_all = lax.all_gather(condition, 'dp', axis=0, tiled=True)  10.8 us
    all_gather x1, blocking collectives, shards(): d_mod_all = lax.all_gather(d_mod_own.astype(bf16), 'dp', axis=0, tiled=True)  9.06 us
  transfers between devices with their start and end apart: 11, of which 6 were waited for; matrix products, arithmetic and copies ran while one was open for 9% of the time, Pallas kernels for 0%

profile of v1, /device:TPU:0, one launch (start us, length us, event | category | flops | bytes accessed | tf_op | source)
XLA Modules:
  0.0 402.7 jit_solution(13563695485046258541)
XLA Ops:
  8.1 10.8 %all-gather.1 = bf16[8,2,768]{2,1,0:T(2,128)(2,1)S(1)} all-gather(bf16[1,2,768]{2,1,0:T(2,128)(2,1)} %bitcast.208), channel_id=1, replica_groups=mesh['dp'=8,'tensor'=4] {'dp'}, dimensions={0}, use_global_device_ids=true | all-gather | bytes 27648 | tf_op jit(solution)/shard_map/all_gather | solution.py:90
  19.8 1.8 pad_maximum_fusion.2
  24.0 45.8 %all-reduce.9.cloned.1.call-done = f32[16,1152]{1,0:T(8,128)} async-done(((f32[16,1152]{1,0:T(8,128)}), f32[16,1152]{1,0:T(8,128)}) %all-reduce.9.cloned.1.call-update) | async-done | bytes 73744
  70.5 13.2 %all_gather.26 = f32[2,4608]{1,0:T(2,128)S(1)} all-gather(f32[2,1152]{1,0:T(2,128)S(1)} %constant_dynamic-slice_fusion.1), channel_id=1, replica_groups=mesh['dp'=8,'tensor'=4] {'tensor'}, dimensions={1}, use_global_device_ids=true | all-gather | bytes 46080 | tf_op jit(solution)/shard_map/all_gather | solution.py:73
  86.9 2.9 convolution_convert_fusion.2
  94.0 2.5 convolution_convert_fusion.1
  97.4 43.9 %all-reduce.5.cloned.1.call-done = bf16[2,256,768]{2,1,0:T(8,128)(2,1)} async-done(((bf16[2,256,768]{2,1,0:T(8,128)(2,1)}), bf16[2,256,768]{2,1,0:T(8,128)(2,1)}) %all-reduce.5.cloned.1.call-update) | async-done | bytes 786448 | tf_op jit(solution)/shard_map/psum | solution.py:53
  143.2 2.4 fusion.31
  150.2 42.8 %all-reduce.7.cloned.1.call-done = bf16[2,256,768]{2,1,0:T(8,128)(2,1)} async-done(((bf16[2,256,768]{2,1,0:T(8,128)(2,1)}), bf16[2,256,768]{2,1,0:T(8,128)(2,1)}) %all-reduce.7.cloned.1.call-update) | async-done | bytes 786448 | tf_op jit(solution)/shard_map/psum | solution.py:53
  193.0 2.0 fusion.24
  195.0 2.3 fusion.10
  203.9 2.6 fusion.26
  206.5 2.1 copy.86
  211.6 1.9 bitcast_convert_fusion.2
  214.6 2.4 copy.88
  217.1 2.3 bitcast_convert_fusion.1
  222.1 4.3 %copy.90 = bf16[768,1536]{1,0:T(8,128)(2,1)} copy(bf16[768,1536]{0,1:T(8,128)(2,1)} %pad_maximum_fusion) | data formatting | bytes 4718592
  226.5 29.4 %reduce-scatter.16.cloned.1.call-done = f32[1152,2]{1,0:T(8,128)} async-done(((f32[4608,2]{1,0:T(8,128)}), f32[1152,2]{1,0:T(8,128)}) %reduce-scatter.16.cloned.1.call-update) | async-done | bytes 9232
  257.2 9.1 %all-gather.2 = bf16[8,2,1152]{2,1,0:T(2,128)(2,1)S(1)} all-gather(bf16[1,2,1152]{2,1,0:T(2,128)(2,1)S(1)} %bitcast.207), channel_id=1, replica_groups=mesh['dp'=8,'tensor'=4] {'dp'}, dimensions={0}, use_global_device_ids=true | all-gather | bytes 41472 | tf_op jit(solution)/shard_map/all_gather | solution.py:177
  266.4 69.4 %all-gather = f32[512,96]{1,0:T(8,128)S(1)} all-gather(f32[16,96]{1,0:T(8,128)S(1)} %fusion.63), channel_id=2, replica_groups=mesh['dp'=8,'tensor'=4] {'dp','tensor'}, dimensions={0}, use_global_device_ids=true | all-gather | bytes 202752 | tf_op jit(solution)/shard_map/all_gather | solution.py:180
  336.6 1.8 fusion.58
  341.3 2.0 multiply_add_fusion.2
  343.4 3.1 reduce-scatter.18.cloned.1.call-done
  349.1 42.9 %reduce-scatter.20.cloned.1.call-done = bf16[96,1536]{1,0:T(8,128)(2,1)} async-done(((bf16[768,1536]{1,0:T(8,128)(2,1)}), bf16[96,1536]{1,0:T(8,128)(2,1)}) %reduce-scatter.20.cloned.1.call-update) | async-done | bytes 294928
  (164 shorter events, 42.0 us)
Async XLA Ops:
  8.0 10.9 %copy-start = (bf16[96,1152]{1,0:T(8,128)(2,1)S(1)}, bf16[96,1152]{1,0:T(8,128)(2,1)}, u32[]{:S(2)}) copy-start(bf16[96,1152]{1,0:T(8,128)(2,1)} %param.10) | copy-start | bytes 663556
  8.0 14.7 %copy-start.28 = (u32[32]{0:T(128)S(1)}, u32[32]{0:T(128)}, u32[]{:S(2)}) copy-start(u32[32]{0:T(128)} %constant.60) | copy-start | bytes 388
  8.0 13.7 %copy-start.16 = (bf16[192,96]{1,0:T(8,128)(2,1)S(1)}, bf16[192,96]{1,0:T(8,128)(2,1)}, u32[]{:S(2)}) copy-start(bf16[192,96]{1,0:T(8,128)(2,1)} %param.12) | copy-start | bytes 110596
  8.0 13.8 %copy-start.12 = (bf16[3,96,192]{2,1,0:T(8,128)(2,1)S(1)}, bf16[3,96,192]{2,1,0:T(8,128)(2,1)}, u32[]{:S(2)}) copy-start(bf16[3,96,192]{2,1,0:T(8,128)(2,1)} %param.11) | copy-start | bytes 331780
  8.0 61.7 %all-reduce.9.cloned.1.call-start = ((), (), s32[]{:S(2)}) async-start(), calls=%async_computation.15 | async-start | bytes 147456
  18.9 66.4 %copy-start.15 = (f32[16,768]{1,0:T(8,128)}, f32[16,768]{1,0:T(8,128)S(1)}, u32[]{:S(2)}) copy-start(f32[16,768]{1,0:T(8,128)S(1)} %reshape.138) | copy-start | bytes 147460
  19.8 64.1 %all-gather.7.cloned.1.call-start = ((), (), s32[]{:S(2)}) async-start(), calls=%async_computation.5 | async-start | bytes 1966080 | tf_op jit(solution)/shard_map/all_gather | solution.py:49
  21.7 65.2 %all-gather.9.cloned.1.call-start = ((), (), s32[]{:S(2)}) async-start(), calls=%async_computation.6 | async-start | bytes 1327104 | tf_op jit(solution)/shard_map/all_gather | solution.py:63
  22.7 118.6 %all-reduce.5.cloned.1.call-start = ((), (), s32[]{:S(2)}) async-start(), calls=%async_computation.7 | async-start | bytes 1572864 | tf_op jit(solution)/shard_map/psum | solution.py:53
  83.8 6.0 %copy-start.22 = (f32[2,1,1,768]{3,0,1,2:T(2,128)}, f32[2,1,1,768]{3,0,1,2:T(2,128)S(1)}, u32[]{:S(2)}) copy-start(f32[2,1,1,768]{3,0,1,2:T(2,128)S(1)} %copy.110) | copy-start | bytes 18436
  83.9 3.0 copy-start.1
  85.3 4.5 %copy-start.20 = (f32[2,256]{1,0:T(2,128)}, f32[2,256]{1,0:T(2,128)S(1)}, u32[]{:S(2)}) copy-start(f32[2,256]{1,0:T(2,128)S(1)} %broadcast_multiply_fusion.3) | copy-start | bytes 6148
  86.9 2.9 copy-start.24
  93.3 3.2 copy-start.13
  94.0 2.6 copy-start.14
  96.5 46.6 %all-gather.11.cloned.1.call-start = ((), (), s32[]{:S(2)}) async-start(), calls=%async_computation.8 | async-start | bytes 2654208 | tf_op jit(solution)/shard_map/all_gather | solution.py:63
  97.3 95.6 %all-reduce.7.cloned.1.call-start = ((), (), s32[]{:S(2)}) async-start(), calls=%async_computation.10 | async-start | bytes 1572864 | tf_op jit(solution)/shard_map/psum | solution.py:53
  143.1 2.4 copy-start.26
  149.9 106.0 %reduce-scatter.16.cloned.1.call-start = ((), (), s32[]{:S(2)}) async-start(), calls=%async_computation.12 | async-start | bytes 2949120
  208.7 129.7 %reduce-scatter.14.cloned.1.call-start = ((), (), s32[]{:S(2)}) async-start(), calls=%async_computation.11 | async-start | bytes 983040 | tf_op jit(solution)/shard_map/reduce_scatter | solution.py:57
  209.4 130.2 %reduce-scatter.12.cloned.1.call-start = ((), (), s32[]{:S(2)}) async-start(), calls=%async_computation.9 | async-start | bytes 983040 | tf_op jit(solution)/shard_map/reduce_scatter | solution.py:57
  210.0 136.4 %reduce-scatter.18.cloned.1.call-start = ((), (), s32[]{:S(2)}) async-start(), calls=%async_computation.13 | async-start | bytes 1327104
  217.1 175.0 %reduce-scatter.20.cloned.1.call-start = ((), (), s32[]{:S(2)}) async-start(), calls=%async_computation.14 | async-start | bytes 2654208
  226.4 109.6 %copy-start.17 = (bf16[2,768]{1,0:T(2,128)(2,1)S(1)}, bf16[2,768]{1,0:T(2,128)(2,1)}, u32[]{:S(2)}) copy-start(bf16[2,768]{1,0:T(2,128)(2,1)} %param.9) | copy-start | bytes 9220
  (20 other events, 32.4 us)
Sparse Core Ops, SparseCore 0:
  19.9 49.8 all-reduce.8
  100.0 30.1 all-gather.10
Sparse Core Ops, SparseCore 1:
  22.4 37.1 all-gather.6
  61.9 22.7 all-gather.8
  96.6 44.7 all-reduce.4
  150.0 42.9 all-reduce.6
  208.8 47.1 reduce-scatter.15
  258.3 23.4 reduce-scatter.13
  284.1 23.1 reduce-scatter.11
  310.7 35.7 reduce-scatter.17
  349.7 42.3 reduce-scatter.19

commit v2 on v1

--- a/solution.py
+++ b/solution.py
@@ -3,7 +3,12 @@
 import jax
 import jax.numpy as jnp
 from jax import lax
+from jax.experimental import pallas as pl
+from jax.experimental.pallas import tpu as pltpu
 from jax.sharding import PartitionSpec as P
+
+MESH = pl.DeviceIdType.MESH
+VMEM = pl.BlockSpec(memory_space=pltpu.VMEM)
 
 HEAD_DIM = 64
 EPS = 1e-06
@@ -49,36 +54,310 @@
     return lax.all_gather(block, "tensor", axis=axis, tiled=True)
 
 
-def reduce_tensor(part):
-    return lax.psum(part.astype(bf16), "tensor").astype(f32)
-
-
-def scatter_tensor(part):
-    return lax.psum_scatter(
-        part.astype(bf16), "tensor", scatter_dimension=1, tiled=True
-    ).astype(f32)
-
-
 def gather_weights(shard):
     return lax.all_gather(shard, "dp", axis=0, tiled=True)
 
 
-def scatter_grads(grads):
-    return lax.psum_scatter(grads.astype(bf16), "dp", scatter_dimension=0, tiled=True).astype(f32)
-
-
-def modulation_of(cond_mine, w_ada):
-    part = jnp.dot(cond_mine, w_ada, preferred_element_type=f32)
-    own = lax.psum_scatter(part, "dp", scatter_dimension=0, tiled=True)
-    return lax.all_gather(own, "tensor", axis=1, tiled=True)
+def greet(axes):
+    barrier = pltpu.get_barrier_semaphore()
+    total = 0
+    for axis in axes:
+        size = lax.axis_size(axis)
+        me = lax.axis_index(axis)
+        for step in range(1, size):
+            pl.semaphore_signal(
+                barrier, inc=1, device_id={axis: lax.rem(me + step, size)}, device_id_type=MESH
+            )
+        total += size - 1
+    pl.semaphore_wait(barrier, total)
+
+
+def start_exchange(axis, source, target, sems):
+    size = lax.axis_size(axis)
+    me = lax.axis_index(axis)
+    copies = []
+    for step in range(1, size):
+        peer = lax.rem(me + step, size)
+        copy = pltpu.make_async_remote_copy(
+            src_ref=source(peer),
+            dst_ref=target,
+            send_sem=sems.at[0, step - 1],
+            recv_sem=sems.at[1, step - 1],
+            device_id={axis: peer},
+            device_id_type=MESH,
+        )
+        copy.start()
+        copies.append(copy)
+    return copies
+
+
+def wait_all(copies):
+    for copy in copies:
+        copy.wait()
+
+
+def exchange(axis, source, target, sems):
+    wait_all(start_exchange(axis, source, target, sems))
+
+
+def sem_pair(axis):
+    return pltpu.SemaphoreType.DMA((2, lax.axis_size(axis) - 1))
+
+
+def call(kernel, outs, scratch, number, *args):
+    return pl.pallas_call(
+        kernel,
+        out_shape=outs,
+        in_specs=[VMEM] * len(args),
+        out_specs=jax.tree.map(lambda _: VMEM, outs),
+        scratch_shapes=scratch,
+        compiler_params=pltpu.CompilerParams(
+            collective_id=number, has_side_effects=True, vmem_limit_bytes=48 * 2**20
+        ),
+    )(*args)
+
+
+def modulation_kernel(cond_ref, w_ref, mod_ref, act_ref, cond_buf, part, recv, own, s0, s1, s2):
+    count = lax.axis_size("dp")
+    me, mine = lax.axis_index("dp"), lax.axis_index("tensor")
+    greet(("dp", "tensor"))
+    copies = start_exchange("dp", lambda peer: cond_ref.at[peer], cond_buf.at[me], s0)
+    cond_buf[me] = cond_ref[me]
+    wait_all(copies)
+
+    @pl.loop(0, count)
+    def _(at):
+        act = silu_value(cond_buf[at]).astype(bf16)
+        act_ref[at] = act.astype(f32)
+        part[at] = jnp.dot(act, w_ref[...], preferred_element_type=f32)
+
+    copies = start_exchange("dp", lambda peer: part.at[peer], recv.at[me], s1)
+    recv[me] = part[me]
+    wait_all(copies)
+    own[...] = jnp.sum(recv[...], axis=0)
+    copies = start_exchange("tensor", lambda peer: own, mod_ref.at[mine], s2)
+    mod_ref[mine] = own[...]
+    wait_all(copies)
+
+
+def modulation_of(condition, w_ada):
+    count, group = lax.axis_size("dp"), lax.axis_size("tensor")
+    rows, width = condition.shape
+    shard_rows, columns = w_ada.shape
+    blocks = condition.astype(f32).reshape(rows, count, shard_rows).transpose(1, 0, 2)
+    mod, act = call(
+        modulation_kernel,
+        (
+            jax.ShapeDtypeStruct((group, rows, columns), f32),
+            jax.ShapeDtypeStruct((count, rows, shard_rows), f32),
+        ),
+        [
+            pltpu.VMEM((count, rows, shard_rows), f32),
+            pltpu.VMEM((count, rows, columns), f32),
+            pltpu.VMEM((count, rows, columns), f32),
+            pltpu.VMEM((rows, columns), f32),
+            sem_pair("dp"),
+            sem_pair("dp"),
+            sem_pair("tensor"),
+        ],
+        1,
+        blocks,
+        w_ada,
+    )
+    mod = mod.transpose(1, 0, 2).reshape(rows, group * columns)
+    return mod, act.reshape(count * rows, shard_rows).astype(bf16)
+
+
+def condition_kernel(
+    part_ref, w_ref, all_ref, act_ref, recv, own, part, terms, gathered, s0, s1, s2, s3
+):
+    count = lax.axis_size("dp")
+    me, mine = lax.axis_index("dp"), lax.axis_index("tensor")
+    greet(("dp", "tensor"))
+    copies = start_exchange("tensor", lambda peer: part_ref.at[peer], recv.at[mine], s0)
+    recv[mine] = part_ref[mine]
+    wait_all(copies)
+    own[...] = jnp.sum(recv[...], axis=0).astype(bf16).astype(f32)
+    copies = start_exchange("dp", lambda peer: own, all_ref.at[me], s1)
+    all_ref[me] = own[...]
+    wait_all(copies)
+
+    @pl.loop(0, count)
+    def _(at):
+        part[at] = lax.dot_general(
+            all_ref[at].astype(bf16),
+            w_ref[...],
+            (((1,), (1,)), ((), ())),
+            preferred_element_type=f32,
+        )
+
+    copies = start_exchange("dp", lambda peer: part.at[peer], terms.at[me], s2)
+    terms[me] = part[me]
+    wait_all(copies)
+    copies = start_exchange("tensor", lambda peer: terms, gathered.at[mine], s3)
+    gathered[mine] = terms[...]
+    wait_all(copies)
+    act_ref[...] = jnp.sum(gathered[...], axis=0)
+
+
+def condition_back(parts, w_ada):
+    count, group = lax.axis_size("dp"), lax.axis_size("tensor")
+    rows = parts.shape[0]
+    shard_rows, columns = w_ada.shape
+    blocks = parts.reshape(rows, group, columns).transpose(1, 0, 2)
+    everyone, act = call(
+        condition_kernel,
+        (
+            jax.ShapeDtypeStruct((count, rows, columns), f32),
+            jax.ShapeDtypeStruct((count, rows, shard_rows), f32),
+        ),
+        [
+            pltpu.VMEM((group, rows, columns), f32),
+            pltpu.VMEM((rows, columns), f32),
+            pltpu.VMEM((count, rows, shard_rows), f32),
+            pltpu.VMEM((count, rows, shard_rows), f32),
+            pltpu.VMEM((group, count, rows, shard_rows), f32),
+            sem_pair("tensor"),
+            sem_pair("dp"),
+            sem_pair("dp"),
+            sem_pair("tensor"),
+        ],
+        2,
+        blocks,
+        w_ada,
+    )
+    everyone = everyone.reshape(count * rows, columns).astype(bf16)
+    return everyone, act.transpose(1, 0, 2).reshape(rows, count * shard_rows)
+
+
+def token_block(ref, at, size):
+    return ref.at[:, pl.ds(pl.multiple_of(at * size, size), size)]
+
+
+def reduce_kernel(part_ref, out_ref, recv, s0, s1):
+    group = lax.axis_size("tensor")
+    mine = lax.axis_index("tensor")
+    size = part_ref.shape[1] // group
+    greet(("tensor",))
+    exchange("tensor", lambda peer: token_block(part_ref, peer, size), recv.at[mine], s0)
+    total = token_block(part_ref, mine, size)[...].astype(f32)
+    for step in range(1, group):
+        total += recv[lax.rem(mine + step, group)].astype(f32)
+    own = token_block(out_ref, mine, size)
+    own[...] = total.astype(bf16)
+    exchange("tensor", lambda peer: own, own, s1)
+
+
+def reduce_tensor(part, number):
+    group = lax.axis_size("tensor")
+    rows, seq, width = part.shape
+    return call(
+        reduce_kernel,
+        jax.ShapeDtypeStruct(part.shape, bf16),
+        [
+            pltpu.VMEM((group, rows, seq // group, width), bf16),
+            sem_pair("tensor"),
+            sem_pair("tensor"),
+        ],
+        number,
+        part.astype(bf16),
+    ).astype(f32)
+
+
+def final_kernel(
+    attn_ref, ffn_ref, grad_ref, attn_out, ffn_out, grad_out, attn_recv, ffn_recv, pair_recv,
+    stage, grad_recv, s0, s1, s2, s3
+):
+    group = lax.axis_size("tensor")
+    count = lax.axis_size("dp")
+    pairs = count // 2
+    me, mine = lax.axis_index("dp"), lax.axis_index("tensor")
+    chip, side = me // 2, lax.rem(me, 2)
+    size = attn_ref.shape[1] // group
+    greet(("dp", "tensor"))
+    pair_copy = pltpu.make_async_remote_copy(
+        src_ref=grad_ref.at[:, 1 - side],
+        dst_ref=pair_recv,
+        send_sem=s0.at[0],
+        recv_sem=s0.at[1],
+        device_id={"dp": 2 * chip + 1 - side},
+        device_id_type=MESH,
+    )
+    pair_copy.start()
+    attn_copies = start_exchange(
+        "tensor", lambda peer: token_block(attn_ref, peer, size), attn_recv.at[mine], s1
+    )
+    ffn_copies = start_exchange(
+        "tensor", lambda peer: token_block(ffn_ref, peer, size), ffn_recv.at[mine], s2
+    )
+    pair_copy.wait()
+    grad_copies = []
+    for step in range(pairs):
+        to = lax.rem(chip + step, pairs) if step else chip
+        total = grad_ref[to, side].astype(f32) + pair_recv[to].astype(f32)
+        if step == 0:
+            grad_out[...] = total
+            continue
+        stage[to] = total.astype(bf16)
+        copy = pltpu.make_async_remote_copy(
+            src_ref=stage.at[to],
+            dst_ref=grad_recv.at[chip],
+            send_sem=s3.at[0, step - 1],
+            recv_sem=s3.at[1, step - 1],
+            device_id={"dp": 2 * to + side},
+            device_id_type=MESH,
+        )
+        copy.start()
+        grad_copies.append(copy)
+    wait_all(grad_copies)
+    for step in range(1, pairs):
+        grad_out[...] += grad_recv[lax.rem(chip + step, pairs)].astype(f32)
+    for copies, source, recv, out in (
+        (attn_copies, attn_ref, attn_recv, attn_out),
+        (ffn_copies, ffn_ref, ffn_recv, ffn_out),
+    ):
+        wait_all(copies)
+        total = token_block(source, mine, size)[...].astype(f32)
+        for step in range(1, group):
+            total += recv[lax.rem(mine + step, group)].astype(f32)
+        out[...] = total
+
+
+def final_sums(attn_part, ffn_part, grads):
+    group, count = lax.axis_size("tensor"), lax.axis_size("dp")
+    rows, seq, width = attn_part.shape
+    depth, columns = grads.shape
+    shard_rows = depth // count
+    tokens = (rows, seq // group, width)
+    return call(
+        final_kernel,
+        (
+            jax.ShapeDtypeStruct(tokens, f32),
+            jax.ShapeDtypeStruct(tokens, f32),
+            jax.ShapeDtypeStruct((shard_rows, columns), f32),
+        ),
+        [
+            pltpu.VMEM((group,) + tokens, bf16),
+            pltpu.VMEM((group,) + tokens, bf16),
+            pltpu.VMEM((count // 2, shard_rows, columns), bf16),
+            pltpu.VMEM((count // 2, shard_rows, columns), bf16),
+            pltpu.VMEM((count // 2, shard_rows, columns), bf16),
+            pltpu.SemaphoreType.DMA((2,)),
+            sem_pair("tensor"),
+            sem_pair("tensor"),
+            pltpu.SemaphoreType.DMA((2, count // 2 - 1)),
+        ],
+        5,
+        attn_part.astype(bf16),
+        ffn_part.astype(bf16),
+        grads.astype(bf16).reshape(count // 2, 2, shard_rows, columns),
+    )
 
 
 def shards(latent_in, condition, w_ada, w_qkv, w_proj, w_up, w_down, out_grad):
     rows, own_tokens, width = latent_in.shape
     scale = HEAD_DIM ** (-0.5)
-    dp_at = lax.axis_index("dp")
     tensor_at = lax.axis_index("tensor")
-    shard_rows = w_ada.shape[0]
     local = w_proj.shape[0]
     heads = local // HEAD_DIM
     units = w_down.shape[0]
@@ -87,10 +366,8 @@
         [w_qkv[0], w_qkv[1], w_qkv[2], w_proj.T], axis=1
     )
     ffn_shard = jnp.concatenate([w_up, w_down.T], axis=1)
-    cond_all = lax.all_gather(condition, "dp", axis=0, tiled=True)
-    cond_act = silu_value(cond_all.astype(f32)).astype(bf16)
-    cond_mine = lax.dynamic_slice_in_dim(cond_act, dp_at * shard_rows, shard_rows, 1)
-    modulation = modulation_of(cond_mine, w_ada).reshape(rows, 6, 1, width)
+    modulation, cond_mine = modulation_of(condition, w_ada)
+    modulation = modulation.reshape(rows, 6, 1, width)
     shift_a, scale_a, gate_a, shift_f, scale_f, gate_f = (modulation[:, i] for i in range(6))
 
     attn_weights = gather_weights(attn_shard)
@@ -115,7 +392,7 @@
     probs = shifted / jnp.sum(shifted, axis=-1, keepdims=True)
     probs_low = probs.astype(bf16)
     mixed = dot("lhqk,lkhe->lqhe", probs_low, values).reshape(rows, seq, local).astype(bf16)
-    attn_out = reduce_tensor(dot("lsd,ed->lse", mixed, proj_t))
+    attn_out = reduce_tensor(dot("lsd,ed->lse", mixed, proj_t), 3)
     resid = tokens + gate_a * attn_out
     normed_f, inverse_f = norm_parts(resid)
     ffn_in = (normed_f * (1.0 + scale_f) + shift_f).astype(bf16)
@@ -124,20 +401,10 @@
     hidden = hidden.astype(bf16)
     d_ffn_out = (gate_f * cotangent).astype(bf16)
     d_hidden_pre = gelu_pull(dot("lse,en->lsn", d_ffn_out, down_t))[0].astype(bf16)
-    d_ffn_in = reduce_tensor(dot("lsn,dn->lsd", d_hidden_pre, up))
+    d_ffn_in = reduce_tensor(dot("lsn,dn->lsd", d_hidden_pre, up), 4)
 
     ffn_part = dot("lsn,en->lse", hidden, down_t)
     d_gate_f = jnp.sum(cotangent * ffn_part, axis=1)
-    ffn_own = scatter_tensor(ffn_part)
-    first = tensor_at * own_tokens
-    resid_own = lax.dynamic_slice_in_dim(resid, first, own_tokens, 1)
-    latent_out = (resid_own + gate_f * ffn_own).astype(bf16)
-
-    grad_ffn = jnp.concatenate(
-        [dot("lsd,lsn->dn", ffn_in, d_hidden_pre), dot("lse,lsn->en", d_ffn_out, hidden)], axis=1
-    )
-    grad_ffn = scatter_grads(grad_ffn)
-
     d_shift_f = jnp.sum(d_ffn_in, axis=1)
     d_scale_f = jnp.sum(d_ffn_in * normed_f, axis=1)
     d_resid = cotangent + norm_back(normed_f, inverse_f, d_ffn_in * (1.0 + scale_f))
@@ -155,13 +422,20 @@
     d_projected = d_projected.reshape(rows, seq, 3 * local).astype(bf16)
     d_attn_part = dot("lse,de->lsd", d_projected, w_in)
 
-    d_attn_own = scatter_tensor(d_attn_part)
-    grad_attn = jnp.concatenate(
-        [dot("lsd,lse->de", attn_in, d_projected), dot("lse,lsd->ed", d_attn_out, mixed)], axis=1
-    )
-    grad_attn = scatter_grads(grad_attn)
-
+    grads = jnp.concatenate(
+        [
+            dot("lsd,lse->de", attn_in, d_projected).astype(bf16),
+            dot("lse,lsd->ed", d_attn_out, mixed).astype(bf16),
+            dot("lsd,lsn->dn", ffn_in, d_hidden_pre).astype(bf16),
+            dot("lse,lsn->en", d_ffn_out, hidden).astype(bf16),
+        ],
+        axis=1,
+    )
+    d_attn_own, ffn_own, grads = final_sums(d_attn_part, ffn_part, grads)
+    grad_attn, grad_ffn = grads[:, : 4 * local], grads[:, 4 * local :]
+    first = tensor_at * own_tokens
     own = lambda value: lax.dynamic_slice_in_dim(value, first, own_tokens, 1)
+    latent_out = (own(resid) + gate_f * ffn_own).astype(bf16)
     grad_latent = own(d_resid) + norm_back(
         own(normed_a), own(inverse_a), d_attn_own * (1.0 + scale_a)
     )
@@ -173,14 +447,8 @@
         [d_shift_a, d_scale_a, d_gate_a * ones, d_shift_f * ones, d_scale_f * ones, d_gate_f],
         axis=1,
     )
-    d_mod_own = lax.psum_scatter(d_modulation, "tensor", scatter_dimension=1, tiled=True)
-    d_mod_all = lax.all_gather(d_mod_own.astype(bf16), "dp", axis=0, tiled=True)
+    d_mod_all, d_act = condition_back(d_modulation, w_ada)
     grad_ada = dot("ld,le->de", cond_mine, d_mod_all)
-    act_part = dot("le,de->ld", d_mod_all, w_ada)
-    act_all = lax.all_gather(act_part, ("dp", "tensor"), axis=0, tiled=False)
-    act_all = act_all.reshape(-1, lax.axis_size("tensor"), cond_all.shape[0], shard_rows)
-    act_own = lax.dynamic_slice_in_dim(act_all, dp_at * rows, rows, 2)
-    d_act = jnp.sum(act_own, axis=1).transpose(1, 0, 2).reshape(rows, width)
     grad_condition = jax.vjp(silu_value, condition.astype(f32))[1](d_act)[0]
 
     grad_qkv = jnp.stack([grad_attn[:, j * local : (j + 1) * local] for j in range(3)], axis=0)

time: 404 us -> 260 us (0.64)
  waiting for transfers between devices: 209 us -> 43.3 us
  Pallas kernels: 0 us -> 154 us
  blocking collectives: 102 us -> 0 us
  local copies, waits for them, and re-layouts: 23 us -> 10.8 us
  matrix products: 28.9 us -> 22.2 us
  other arithmetic: 21.2 us -> 14.8 us
    pallas_call x0 -> x5, Pallas kernels: none -> 154 us  [call(): pl.pallas_call(kernel, out_shape=outs, in_specs=[VMEM] * len(args), out_s...]
    unnamed x15 -> x3, waiting for transfers between devices: 123 us -> 0.05 us
    all_gather x4 -> x0, blocking collectives: 102 us -> none  [the longest x1 69.4 us: shards(): act_all = lax.all_gather(act_part, ('dp', 'tensor'), axis=0, tiled=False)]
    psum x2 -> x0, waiting for transfers between devices: 86.7 us -> none  [reduce_tensor(): return lax.psum(part.astype(bf16), 'tensor').astype(f32)]
    all_gather x2, waiting for transfers between devices: 0.05 us -> 22.4 us  [gather_weights(): return lax.all_gather(shard, 'dp', axis=0, tiled=True)]
    all_gather x1, waiting for transfers between devices: 0.03 us -> 20.8 us  [gather_tensor(): return lax.all_gather(block, 'tensor', axis=axis, tiled=True)]
    unnamed x86 -> x38, local copies, waits for them, and re-layouts: 22 us -> 2.77 us
    concatenate x0 -> x1, local copies, waits for them, and re-layouts: none -> 5.9 us  [shards(): jnp.concatenate([dot('lsd,lse->de', attn_in, d_projected).astype(bf16), d...]
  transfers between devices with their start and end apart: 11 -> 3, of which waited for: 6 -> 2; matrix products, arithmetic and copies ran while one was open for 9% -> 5% of each run, Pallas kernels for 0% -> 20%
where the time goes in v2:
time: 260 us; the launch traced here: 259 us
  Pallas kernels  154 us (59%)
  waiting for transfers between devices  43.3 us (17%)
  matrix products  22.2 us (9%)
  other arithmetic  14.8 us (6%)
  between operations  14.2 us (5%)
  local copies, waits for them, and re-layouts  10.8 us (4%)
    pallas_call x5, Pallas kernels, call(): pl.pallas_call(kernel, out_shape=outs, in_specs=[VMEM] * len(args), out_s...  154 us
    all_gather x2, waiting for transfers between devices, gather_weights(): return lax.all_gather(shard, 'dp', axis=0, tiled=True)  22.4 us
    dot_general x18, matrix products, dot(): return jnp.einsum(form, left, right, preferred_element_type=f32)  21.5 us
    all_gather x1, waiting for transfers between devices, gather_tensor(): return lax.all_gather(block, 'tensor', axis=axis, tiled=True)  20.8 us
    concatenate x1, local copies, waits for them, and re-layouts, shards(): jnp.concatenate([dot('lsd,lse->de', attn_in, d_projected).astype(bf16), d...  5.9 us
  transfers between devices with their start and end apart: 3, of which 2 were waited for; matrix products, arithmetic and copies ran while one was open for 5% of the time, Pallas kernels for 20%

profile of v2, /device:TPU:0, one launch (start us, length us, event | category | flops | bytes accessed | tf_op | source)
XLA Modules:
  0.0 259.2 jit_solution(16507575435043667643)
XLA Ops:
  7.3 1.9 pad_maximum_fusion.1
  9.3 0.9 copy.52
  12.8 17.2 %shard_map.143 = (f32[4,2,1152]{2,1,0:T(2,128)S(1)}, f32[8,2,96]{2,1,0:T(2,128)S(1)}) custom-call(f32[8,2,96]{2,1,0:T(2,128)S(1)} %bitcast.174, bf16[96,1152]{1,0:T(8,128)(2,1)S(1)} %copy-done), custom_call_target="tpu_custom_call" | custom-call | tf_op jit(solution)/shard_map/pallas_call | solution.py:108
  30.0 20.8 %all-gather.4.cloned.1.call-done = bf16[2,2,256,768]{3,2,1,0:T(8,128)(2,1)} async-done(((bf16[2,2,64,768]{3,2,1,0:T(8,128)(2,1)}), bf16[2,2,256,768]{3,2,1,0:T(8,128)(2,1)}) %all-gather.4.cloned.1.call-update) | async-done | bytes 1572880 | tf_op jit(solution)/shard_map/all_gather | solution.py:54
  50.8 1.4 convert_reduce_fusion.1
  52.3 1.5 fusion.9
  53.8 22.4 %all-gather.6.cloned.1.call-done = bf16[768,768]{1,0:T(8,128)(2,1)} async-done(((bf16[96,768]{1,0:T(8,128)(2,1)}), bf16[768,768]{1,0:T(8,128)(2,1)}) %all-gather.6.cloned.1.call-update) | async-done | bytes 1179664 | tf_op jit(solution)/shard_map/all_gather | solution.py:58
  76.2 2.0 convolution_convert_fusion.2
  80.1 1.7 convolution_convert_fusion.1.part_ref
  81.8 35.6 %shard_map.144 = bf16[2,256,768]{2,1,0:T(8,128)(2,1)S(1)} custom-call(bf16[2,256,768]{2,1,0:T(8,128)(2,1)S(1)} %convolution_convert_fusion.1.part_ref), custom_call_target="tpu_custom_call" | custom-call | tf_op jit(solution)/shard_map/pallas_call | solution.py:108
  118.2 2.4 fusion.31
  120.6 1.7 fusion.17
  123.2 38.6 %shard_map.145 = bf16[2,256,768]{2,1,0:T(8,128)(2,1)S(1)} custom-call(bf16[2,256,768]{2,1,0:T(8,128)(2,1)S(1)} %convolution_convert_fusion.part_ref), custom_call_target="tpu_custom_call" | custom-call | tf_op jit(solution)/shard_map/pallas_call | solution.py:108
  163.5 2.0 convolution_convert_fusion.3
  167.3 1.0 bitcast_convert_fusion.1
  168.8 1.3 bitcast_convert_fusion
  171.0 2.1 pad_maximum_fusion
  173.0 5.9 %copy.65 = bf16[768,2304]{1,0:T(8,128)(2,1)} copy(bf16[768,2304]{0,1:T(8,128)(2,1)} %pad_maximum_fusion) | data formatting | bytes 7077888 | tf_op jit(solution)/shard_map/concatenate | solution.py:425
  179.0 2.0 fusion.41
  181.0 2.7 %fusion.26 = (f32[2,768]{1,0:T(2,128)S(1)}, f32[2,768]{1,0:T(2,128)S(1)}, f32[2,768]{1,0:T(2,128)S(1)}, f32[2,256,768]{2,1,0:T(8,128)S(1)}, bf16[2,256,768]{2,1,...) fusion(bf16[2,2,256,768]{3,2,1,0:T(8,128)(2,1)S(1)} %copy-done.5, f32[2,256,768]{2,1,0:T(8,128)S(1)} %fusion.41, ...), kind=kOutput, calls=%fused_computation.46 | convolution fusion | flops 611839488 | bytes 9066496 | tf_op jit(solution)/shard_map/lsn,en->lse/dot_general | solution.py:50
  183.7 41.4 %shard_map.146 = (f32[2,64,768]{2,1,0:T(8,128)S(1)}, f32[2,64,768]{2,1,0:T(8,128)S(1)}, f32[96,2304]{1,0:T(8,128)S(1)}) custom-call(bf16[2,256,768]{2,1,0:T(8,128)(2,1)S(1)} %get-tuple-element.60.attn_ref, bf16[2,256,768]{2,1,0:T(8,128)(2,1)S(1)} %get-tuple-element.61.ffn_ref, bf16[4,2,96,2304]{3,2,1,0:T(8,128)(2,1)} %bitcast.176), custom_call_target="tpu_custom_call" | custom-call | tf_op jit(solution)/shard_map/pallas_call | solution.py:108
  226.4 21.0 %shard_map.147 = (f32[8,2,1152]{2,1,0:T(2,128)S(1)}, f32[8,2,96]{2,1,0:T(2,128)S(1)}) custom-call(f32[4,2,1152]{2,1,0:T(2,128)S(1)} %bitcast.172, bf16[96,1152]{1,0:T(8,128)(2,1)S(1)} %copy-done), custom_call_target="tpu_custom_call" | custom-call | tf_op jit(solution)/shard_map/pallas_call | solution.py:108
  248.8 1.0 convolution_bitcast_fusion
  250.6 2.1 multiply_add_fusion.2
  (88 shorter events, 14.4 us)
Async XLA Ops:
  7.2 4.7 %copy-start.11 = (bf16[768,96]{0,1:T(8,128)(2,1)S(1)}, bf16[768,96]{0,1:T(8,128)(2,1)}, u32[]{:S(2)}) copy-start(bf16[768,96]{0,1:T(8,128)(2,1)} %param.14) | copy-start | bytes 442372
  7.2 4.7 %copy-start.12 = (bf16[96,768]{1,0:T(8,128)(2,1)S(1)}, bf16[96,768]{1,0:T(8,128)(2,1)}, u32[]{:S(2)}) copy-start(bf16[96,768]{1,0:T(8,128)(2,1)} %param.13) | copy-start | bytes 442372
  7.2 5.5 %copy-start.13 = (bf16[2,768]{1,0:T(2,128)(2,1)S(1)}, bf16[2,768]{1,0:T(2,128)(2,1)}, u32[]{:S(2)}) copy-start(bf16[2,768]{1,0:T(2,128)(2,1)} %param.9) | copy-start | bytes 9220
  7.2 5.6 %copy-start = (bf16[96,1152]{1,0:T(8,128)(2,1)S(1)}, bf16[96,1152]{1,0:T(8,128)(2,1)}, u32[]{:S(2)}) copy-start(bf16[96,1152]{1,0:T(8,128)(2,1)} %w_ref.3) | copy-start | bytes 663556
  7.2 43.6 %all-gather.4.cloned.1.call-start = ((), (), s32[]{:S(2)}) async-start(), calls=%async_computation | async-start | bytes 1966080 | tf_op jit(solution)/shard_map/all_gather | solution.py:54
  9.2 67.0 %all-gather.6.cloned.1.call-start = ((), (), s32[]{:S(2)}) async-start(), calls=%async_computation.1 | async-start | bytes 1327104 | tf_op jit(solution)/shard_map/all_gather | solution.py:58
  11.8 106.3 %all-gather.8.cloned.1.call-start = ((), (), s32[]{:S(2)}) async-start(), calls=%async_computation.2 | async-start | bytes 2654208 | tf_op jit(solution)/shard_map/all_gather | solution.py:58
  50.8 25.4 %copy-start.2 = (bf16[2,2,256,768]{3,2,1,0:T(8,128)(2,1)S(1)}, bf16[2,2,256,768]{3,2,1,0:T(8,128)(2,1)}, u32[]{:S(2)}) copy-start(bf16[2,2,256,768]{3,2,1,0:T(8,128)(2,1)} %all-gather.4.cloned.1.call-done) | copy-start | bytes 4718596
  78.9 1.2 copy-start.8
  80.1 37.4 %copy-start.3 = (bf16[2,2,256,768]{3,2,1,0:T(8,128)(2,1)S(1)}, bf16[2,2,256,768]{3,2,1,0:T(8,128)(2,1)}, u32[]{:S(2)}) copy-start(bf16[2,2,256,768]{3,2,1,0:T(8,128)(2,1)} %all-gather.4.cloned.1.call-done) | copy-start | bytes 4718596
  118.1 2.4 copy-start.4
  118.2 2.5 copy-start.14
  120.5 48.2 %copy-start.15 = (f32[2,256,768]{2,1,0:T(8,128)}, f32[2,256,768]{2,1,0:T(8,128)S(1)}, u32[]{:S(2)}) copy-start(f32[2,256,768]{2,1,0:T(8,128)S(1)} %fusion.31) | copy-start | bytes 4718596
  163.5 4.8 %copy-start.1 = (f32[2,256,768]{2,1,0:T(8,128)}, f32[2,256,768]{2,1,0:T(8,128)S(1)}, u32[]{:S(2)}) copy-start(f32[2,256,768]{2,1,0:T(8,128)S(1)} %get-tuple-element.56) | copy-start | bytes 4718596
  163.5 2.1 copy-start.9
  168.8 1.3 copy-start.7
  173.0 5.9 %copy-start.6 = (bf16[768,768]{1,0:T(8,128)(2,1)S(1)}, bf16[768,768]{1,0:T(8,128)(2,1)}, u32[]{:S(2)}) copy-start(bf16[768,768]{1,0:T(8,128)(2,1)} %all-gather.6.cloned.1.call-done) | copy-start | bytes 3538948
  179.0 2.1 copy-start.5
  179.0 2.1 copy-start.16
  183.7 42.4 %copy-start.10 = (f32[2,256,768]{2,1,0:T(8,128)}, f32[2,256,768]{2,1,0:T(8,128)S(1)}, u32[]{:S(2)}) copy-start(f32[2,256,768]{2,1,0:T(8,128)S(1)} %get-tuple-element.59) | copy-start | bytes 4718596
Sparse Core Ops, SparseCore 0:
  10.2 40.6 all-gather.3
  53.3 22.8 all-gather.5
  78.7 29.0 all-gather.7

commit v3 on v2

--- a/solution.py
+++ b/solution.py
@@ -117,12 +117,19 @@
     )(*args)
 
 
-def modulation_kernel(cond_ref, w_ref, mod_ref, act_ref, cond_buf, part, recv, own, s0, s1, s2):
+def modulation_kernel(
+    cond_ref, w_ref, x_ref, shard_ref, mod_ref, act_ref, x_all, w_all,
+    cond_buf, part, recv, own, s0, s1, s2, s3, s4, s5
+):
     count = lax.axis_size("dp")
     me, mine = lax.axis_index("dp"), lax.axis_index("tensor")
     greet(("dp", "tensor"))
     copies = start_exchange("dp", lambda peer: cond_ref.at[peer], cond_buf.at[me], s0)
+    x_own = token_block(x_all, mine, x_ref.shape[1])
+    x_copies = start_exchange("tensor", lambda peer: x_ref, x_own, s3)
     cond_buf[me] = cond_ref[me]
+    x_own[...] = x_ref[...]
+    w_all[me] = shard_ref[...]
     wait_all(copies)
 
     @pl.loop(0, count)
@@ -133,23 +140,52 @@
 
     copies = start_exchange("dp", lambda peer: part.at[peer], recv.at[me], s1)
     recv[me] = part[me]
+    pairs = count // 2
+    chip, side = me // 2, lax.rem(me, 2)
+    sibling = 2 * chip + 1 - side
+
+    def send(source, at, to, sems, number):
+        copy = pltpu.make_async_remote_copy(
+            src_ref=source,
+            dst_ref=w_all.at[at],
+            send_sem=sems.at[0, number],
+            recv_sem=sems.at[1, number],
+            device_id={"dp": to},
+            device_id_type=MESH,
+        )
+        copy.start()
+        return copy
+
+    far = [
+        send(shard_ref, me, 2 * lax.rem(chip + step, pairs) + side, s4, step)
+        for step in range(1, pairs)
+    ]
+    near = [send(shard_ref, me, sibling, s5, 0)]
     wait_all(copies)
     own[...] = jnp.sum(recv[...], axis=0)
     copies = start_exchange("tensor", lambda peer: own, mod_ref.at[mine], s2)
     mod_ref[mine] = own[...]
+    for step in range(1, pairs):
+        far[step - 1].wait()
+        came = 2 * lax.rem(chip + pairs - step, pairs) + side
+        near.append(send(w_all.at[came], came, sibling, s5, step))
+    wait_all(near)
     wait_all(copies)
-
-
-def modulation_of(condition, w_ada):
+    wait_all(x_copies)
+
+
+def modulation_of(condition, w_ada, block, shard):
     count, group = lax.axis_size("dp"), lax.axis_size("tensor")
     rows, width = condition.shape
     shard_rows, columns = w_ada.shape
     blocks = condition.astype(f32).reshape(rows, count, shard_rows).transpose(1, 0, 2)
-    mod, act = call(
+    mod, act, x_all, w_all = call(
         modulation_kernel,
         (
             jax.ShapeDtypeStruct((group, rows, columns), f32),
             jax.ShapeDtypeStruct((count, rows, shard_rows), f32),
+            jax.ShapeDtypeStruct((rows, group * block.shape[1], width), bf16),
+            jax.ShapeDtypeStruct((count,) + shard.shape, bf16),
         ),
         [
             pltpu.VMEM((count, rows, shard_rows), f32),
@@ -159,75 +195,19 @@
             sem_pair("dp"),
             sem_pair("dp"),
             sem_pair("tensor"),
+            sem_pair("tensor"),
+            pltpu.SemaphoreType.DMA((2, count // 2)),
+            pltpu.SemaphoreType.DMA((2, count // 2)),
         ],
         1,
         blocks,
         w_ada,
+        block,
+        shard,
     )
     mod = mod.transpose(1, 0, 2).reshape(rows, group * columns)
-    return mod, act.reshape(count * rows, shard_rows).astype(bf16)
-
-
-def condition_kernel(
-    part_ref, w_ref, all_ref, act_ref, recv, own, part, terms, gathered, s0, s1, s2, s3
-):
-    count = lax.axis_size("dp")
-    me, mine = lax.axis_index("dp"), lax.axis_index("tensor")
-    greet(("dp", "tensor"))
-    copies = start_exchange("tensor", lambda peer: part_ref.at[peer], recv.at[mine], s0)
-    recv[mine] = part_ref[mine]
-    wait_all(copies)
-    own[...] = jnp.sum(recv[...], axis=0).astype(bf16).astype(f32)
-    copies = start_exchange("dp", lambda peer: own, all_ref.at[me], s1)
-    all_ref[me] = own[...]
-    wait_all(copies)
-
-    @pl.loop(0, count)
-    def _(at):
-        part[at] = lax.dot_general(
-            all_ref[at].astype(bf16),
-            w_ref[...],
-            (((1,), (1,)), ((), ())),
-            preferred_element_type=f32,
-        )
-
-    copies = start_exchange("dp", lambda peer: part.at[peer], terms.at[me], s2)
-    terms[me] = part[me]
-    wait_all(copies)
-    copies = start_exchange("tensor", lambda peer: terms, gathered.at[mine], s3)
-    gathered[mine] = terms[...]
-    wait_all(copies)
-    act_ref[...] = jnp.sum(gathered[...], axis=0)
-
-
-def condition_back(parts, w_ada):
-    count, group = lax.axis_size("dp"), lax.axis_size("tensor")
-    rows = parts.shape[0]
-    shard_rows, columns = w_ada.shape
-    blocks = parts.reshape(rows, group, columns).transpose(1, 0, 2)
-    everyone, act = call(
-        condition_kernel,
-        (
-            jax.ShapeDtypeStruct((count, rows, columns), f32),
-            jax.ShapeDtypeStruct((count, rows, shard_rows), f32),
-        ),
-        [
-            pltpu.VMEM((group, rows, columns), f32),
-            pltpu.VMEM((rows, columns), f32),
-            pltpu.VMEM((count, rows, shard_rows), f32),
-            pltpu.VMEM((count, rows, shard_rows), f32),
-            pltpu.VMEM((group, count, rows, shard_rows), f32),
-            sem_pair("tensor"),
-            sem_pair("dp"),
-            sem_pair("dp"),
-            sem_pair("tensor"),
-        ],
-        2,
-        blocks,
-        w_ada,
-    )
-    everyone = everyone.reshape(count * rows, columns).astype(bf16)
-    return everyone, act.transpose(1, 0, 2).reshape(rows, count * shard_rows)
+    act = act.reshape(count * rows, shard_rows).astype(bf16)
+    return mod, act, x_all, w_all.reshape(count * shard.shape[0], shard.shape[1])
 
 
 def token_block(ref, at, size):
@@ -265,8 +245,9 @@
 
 
 def final_kernel(
-    attn_ref, ffn_ref, grad_ref, attn_out, ffn_out, grad_out, attn_recv, ffn_recv, pair_recv,
-    stage, grad_recv, s0, s1, s2, s3
+    attn_ref, ffn_ref, grad_ref, part_ref, w_ref, attn_out, ffn_out, grad_out, all_ref, act_ref,
+    attn_recv, ffn_recv, pair_recv, stage, grad_recv, recv_mod, own, part, terms, gathered,
+    s0, s1, s2, s3, m0, m1, m2, m3
 ):
     group = lax.axis_size("tensor")
     count = lax.axis_size("dp")
@@ -275,6 +256,8 @@
     chip, side = me // 2, lax.rem(me, 2)
     size = attn_ref.shape[1] // group
     greet(("dp", "tensor"))
+    copies = start_exchange("tensor", lambda peer: part_ref.at[peer], recv_mod.at[mine], m0)
+    recv_mod[mine] = part_ref[mine]
     pair_copy = pltpu.make_async_remote_copy(
         src_ref=grad_ref.at[:, 1 - side],
         dst_ref=pair_recv,
@@ -290,6 +273,23 @@
     ffn_copies = start_exchange(
         "tensor", lambda peer: token_block(ffn_ref, peer, size), ffn_recv.at[mine], s2
     )
+    wait_all(copies)
+    own[...] = jnp.sum(recv_mod[...], axis=0).astype(bf16).astype(f32)
+    copies = start_exchange("dp", lambda peer: own, all_ref.at[me], m1)
+    all_ref[me] = own[...]
+    wait_all(copies)
+
+    @pl.loop(0, count)
+    def _(at):
+        part[at] = lax.dot_general(
+            all_ref[at].astype(bf16),
+            w_ref[...],
+            (((1,), (1,)), ((), ())),
+            preferred_element_type=f32,
+        )
+
+    copies = start_exchange("dp", lambda peer: part.at[peer], terms.at[me], m2)
+    terms[me] = part[me]
     pair_copy.wait()
     grad_copies = []
     for step in range(pairs):
@@ -309,6 +309,9 @@
         )
         copy.start()
         grad_copies.append(copy)
+    wait_all(copies)
+    last_copies = start_exchange("tensor", lambda peer: terms, gathered.at[mine], m3)
+    gathered[mine] = terms[...]
     wait_all(grad_copies)
     for step in range(1, pairs):
         grad_out[...] += grad_recv[lax.rem(chip + step, pairs)].astype(f32)
@@ -321,20 +324,25 @@
         for step in range(1, group):
             total += recv[lax.rem(mine + step, group)].astype(f32)
         out[...] = total
-
-
-def final_sums(attn_part, ffn_part, grads):
+    wait_all(last_copies)
+    act_ref[...] = jnp.sum(gathered[...], axis=0)
+
+
+def final_sums(attn_part, ffn_part, grads, parts, w_ada):
     group, count = lax.axis_size("tensor"), lax.axis_size("dp")
     rows, seq, width = attn_part.shape
     depth, columns = grads.shape
     shard_rows = depth // count
     tokens = (rows, seq // group, width)
-    return call(
+    mod_columns = w_ada.shape[1]
+    attn_own, ffn_own, grads, everyone, act = call(
         final_kernel,
         (
             jax.ShapeDtypeStruct(tokens, f32),
             jax.ShapeDtypeStruct(tokens, f32),
             jax.ShapeDtypeStruct((shard_rows, columns), f32),
+            jax.ShapeDtypeStruct((count, rows, mod_columns), f32),
+            jax.ShapeDtypeStruct((count, rows, shard_rows), f32),
         ),
         [
             pltpu.VMEM((group,) + tokens, bf16),
@@ -342,16 +350,30 @@
             pltpu.VMEM((count // 2, shard_rows, columns), bf16),
             pltpu.VMEM((count // 2, shard_rows, columns), bf16),
             pltpu.VMEM((count // 2, shard_rows, columns), bf16),
+            pltpu.VMEM((group, rows, mod_columns), f32),
+            pltpu.VMEM((rows, mod_columns), f32),
+            pltpu.VMEM((count, rows, shard_rows), f32),
+            pltpu.VMEM((count, rows, shard_rows), f32),
+            pltpu.VMEM((group, count, rows, shard_rows), f32),
             pltpu.SemaphoreType.DMA((2,)),
             sem_pair("tensor"),
             sem_pair("tensor"),
             pltpu.SemaphoreType.DMA((2, count // 2 - 1)),
+            sem_pair("tensor"),
+            sem_pair("dp"),
+            sem_pair("dp"),
+            sem_pair("tensor"),
         ],
         5,
         attn_part.astype(bf16),
         ffn_part.astype(bf16),
         grads.astype(bf16).reshape(count // 2, 2, shard_rows, columns),
-    )
+        parts.reshape(rows, group, mod_columns).transpose(1, 0, 2),
+        w_ada,
+    )
+    everyone = everyone.reshape(count * rows, mod_columns).astype(bf16)
+    d_act = act.transpose(1, 0, 2).reshape(rows, count * shard_rows)
+    return attn_own, ffn_own, grads, everyone, d_act
 
 
 def shards(latent_in, condition, w_ada, w_qkv, w_proj, w_up, w_down, out_grad):
@@ -366,20 +388,20 @@
         [w_qkv[0], w_qkv[1], w_qkv[2], w_proj.T], axis=1
     )
     ffn_shard = jnp.concatenate([w_up, w_down.T], axis=1)
-    modulation, cond_mine = modulation_of(condition, w_ada)
+    modulation, cond_mine, tokens, attn_weights = modulation_of(
+        condition, w_ada, latent_in, attn_shard
+    )
     modulation = modulation.reshape(rows, 6, 1, width)
     shift_a, scale_a, gate_a, shift_f, scale_f, gate_f = (modulation[:, i] for i in range(6))
 
-    attn_weights = gather_weights(attn_shard)
     w_in = attn_weights[:, : 3 * local]
     proj_t = attn_weights[:, 3 * local :]
-    both = gather_tensor(jnp.stack([latent_in, out_grad], axis=0), 2)
+    cotangent = gather_tensor(out_grad, 1).astype(f32)
     ffn_weights = gather_weights(ffn_shard)
     up = ffn_weights[:, :units]
     down_t = ffn_weights[:, units:]
 
-    tokens = both[0].astype(f32)
-    cotangent = both[1].astype(f32)
+    tokens = tokens.astype(f32)
     seq = tokens.shape[1]
 
     normed_a, inverse_a = norm_parts(tokens)
@@ -431,7 +453,16 @@
         ],
         axis=1,
     )
-    d_attn_own, ffn_own, grads = final_sums(d_attn_part, ffn_part, grads)
+    d_shift_a = jnp.sum(d_attn_part, axis=1)
+    d_scale_a = jnp.sum(d_attn_part * normed_a, axis=1)
+    ones = jnp.where(tensor_at == 0, 1.0, 0.0)
+    d_modulation = jnp.concatenate(
+        [d_shift_a, d_scale_a, d_gate_a * ones, d_shift_f * ones, d_scale_f * ones, d_gate_f],
+        axis=1,
+    )
+    d_attn_own, ffn_own, grads, d_mod_all, d_act = final_sums(
+        d_attn_part, ffn_part, grads, d_modulation, w_ada
+    )
     grad_attn, grad_ffn = grads[:, : 4 * local], grads[:, 4 * local :]
     first = tensor_at * own_tokens
     own = lambda value: lax.dynamic_slice_in_dim(value, first, own_tokens, 1)
@@ -440,14 +471,6 @@
         own(normed_a), own(inverse_a), d_attn_own * (1.0 + scale_a)
     )
 
-    d_shift_a = jnp.sum(d_attn_part, axis=1)
-    d_scale_a = jnp.sum(d_attn_part * normed_a, axis=1)
-    ones = jnp.where(tensor_at == 0, 1.0, 0.0)
-    d_modulation = jnp.concatenate(
-        [d_shift_a, d_scale_a, d_gate_a * ones, d_shift_f * ones, d_scale_f * ones, d_gate_f],
-        axis=1,
-    )
-    d_mod_all, d_act = condition_back(d_modulation, w_ada)
     grad_ada = dot("ld,le->de", cond_mine, d_mod_all)
     grad_condition = jax.vjp(silu_value, condition.astype(f32))[1](d_act)[0]
 

time: 260 us -> 217 us (0.83)
  waiting for transfers between devices: 43.3 us -> 0.02 us
  blocking collectives: 0 us -> 21.7 us
  Pallas kernels: 154 us -> 135 us
  local copies, waits for them, and re-layouts: 10.8 us -> 14.6 us
  other arithmetic: 14.8 us -> 11.1 us
    all_gather x2 -> x1, waiting for transfers between devices: 22.4 us -> 0.01 us  [gather_weights(): return lax.all_gather(shard, 'dp', axis=0, tiled=True)]
    all_gather x0 -> x1, blocking collectives: none -> 21.7 us  [gather_tensor(): return lax.all_gather(block, 'tensor', axis=axis, tiled=True)]
    all_gather x1 -> x0, waiting for transfers between devices: 20.8 us -> none  [gather_tensor(): return lax.all_gather(block, 'tensor', axis=axis, tiled=True)]
    pallas_call x5 -> x4, Pallas kernels: 154 us -> 135 us  [call(): pl.pallas_call(kernel, out_shape=outs, in_specs=[VMEM] * len(args), out_s...]
    dot_general x18, matrix products: 21.5 us -> 18.2 us  [dot(): return jnp.einsum(form, left, right, preferred_element_type=f32)]
    unnamed x38 -> x34, local copies, waits for them, and re-layouts: 2.77 us -> 6.02 us
  transfers between devices with their start and end apart: 3 -> 1, of which waited for: 2 -> 0; matrix products, arithmetic and copies ran while one was open for 5% -> 4% of each run, Pallas kernels for 20% -> 27%
where the time goes in v3:
time: 217 us; the launch traced here: 216 us
  Pallas kernels  135 us (62%)
  blocking collectives  21.7 us (10%)
  matrix products  20 us (9%)
  local copies, waits for them, and re-layouts  14.6 us (7%)
  between operations  14.5 us (7%)
  other arithmetic  11.1 us (5%)
    pallas_call x4, Pallas kernels, call(): pl.pallas_call(kernel, out_shape=outs, in_specs=[VMEM] * len(args), out_s...  135 us
    all_gather x1, blocking collectives, gather_tensor(): return lax.all_gather(block, 'tensor', axis=axis, tiled=True)  21.7 us
    dot_general x18, matrix products, dot(): return jnp.einsum(form, left, right, preferred_element_type=f32)  18.2 us
    unnamed x34, local copies, waits for them, and re-layouts  6.02 us
    concatenate x1, local copies, waits for them, and re-layouts, shards(): jnp.concatenate([dot('lsd,lse->de', attn_in, d_projected).astype(bf16), d...  5.78 us
  transfers between devices with their start and end apart: 1, of which 0 were waited for; matrix products, arithmetic and copies ran while one was open for 4% of the time, Pallas kernels for 27%

profile of v3, /device:TPU:0, one launch (start us, length us, event | category | flops | bytes accessed | tf_op | source)
XLA Modules:
  0.0 216.4 jit_solution(222068077285543126)
XLA Ops:
  7.2 1.8 pad_maximum_fusion.2
  9.9 0.9 copy.33
  10.7 0.9 slice_bitcast_fusion.32
  11.7 25.6 %shard_map.143 = (f32[4,2,1152]{2,1,0:T(2,128)S(1)}, f32[8,2,96]{2,1,0:T(2,128)S(1)}, bf16[2,256,768]{2,1,0:T(8,128)(2,1)S(1)}, bf16[8,96,768]{2,1,0:T(8,128)(2,1)S(1)}) custom-call(f32[8,2,96]{2,1,0:T(2,128)S(1)} %bitcast.144, bf16[96,1152]{1,0:T(8,128)(2,1)S(1)} %copy-done, bf16[2,64,768]{2,1,0:T(8,128)(2,1)S(1)} %copy-done.3, ...), custom_call_target="tpu_custom_call" | custom-call | tf_op jit(solution)/shard_map/pallas_call | solution.py:108
  38.0 0.9 convolution_convert_fusion.2
  38.9 1.8 fusion.44
  40.7 1.7 convolution_convert_fusion.5
  43.0 33.4 %shard_map.144 = bf16[2,256,768]{2,1,0:T(8,128)(2,1)S(1)} custom-call(bf16[2,256,768]{2,1,0:T(8,128)(2,1)S(1)} %convolution_convert_fusion.1.part_ref), custom_call_target="tpu_custom_call" | custom-call | tf_op jit(solution)/shard_map/pallas_call | solution.py:108
  76.9 1.2 copy-done.4
  78.4 21.7 %all_gather.6 = bf16[2,256,768]{2,1,0:T(8,128)(2,1)S(1)} all-gather(bf16[2,64,768]{2,1,0:T(8,128)(2,1)S(1)} %copy-done.12), channel_id=1, replica_groups=mesh['dp'=8,'tensor'=4] {'tensor'}, dimensions={1}, use_global_device_ids=true | all-gather | bytes 983040 | tf_op jit(solution)/shard_map/all_gather | solution.py:54
  100.1 2.6 %fusion.28 = f32[2,256,768]{2,1,0:T(8,128)S(1)} fusion(bf16[768,1536]{1,0:T(8,128)(2,1)} %all-gather.2.cloned.1.call-done, f32[2,256,768]{2,1,0:T(8,128)} %copy-done.4, f32[2,768]{1,0:T(2,128)S(1)} %get-tuple-element.70, f32[2,768]{1,0:T(2,128)S(1)} %get-tuple-element.71, f32[2,256]{1,0:T(2,128)S(1)} %add_rsqrt_fusion, ...), kind=kOutput, calls=%fused_computation.70 | convolution fusion | flops 605945856 | bytes 4341760 | tf_op jit(solution)/shard_map/lsd,dn->lsn/dot_general | solution.py:50
  102.7 1.1 bitcast_convert_fusion
  104.4 1.7 fusion.15
  106.9 29.4 %shard_map.145 = bf16[2,256,768]{2,1,0:T(8,128)(2,1)S(1)} custom-call(bf16[2,256,768]{2,1,0:T(8,128)(2,1)S(1)} %convolution_convert_fusion.part_ref), custom_call_target="tpu_custom_call" | custom-call | tf_op jit(solution)/shard_map/pallas_call | solution.py:108
  137.1 1.5 fusion.17
  139.0 1.5 copy-done.2
  141.1 1.0 bitcast_convert_fusion.1
  145.9 2.1 multiply_reduce_fusion
  148.0 2.1 pad_maximum_fusion
  150.0 5.8 %copy.46 = bf16[768,2304]{1,0:T(8,128)(2,1)} copy(bf16[768,2304]{0,1:T(8,128)(2,1)} %pad_maximum_fusion) | data formatting | bytes 7077888 | tf_op jit(solution)/shard_map/concatenate | solution.py:447
  155.9 46.1 %shard_map.146 = (f32[2,64,768]{2,1,0:T(8,128)S(1)}, f32[2,64,768]{2,1,0:T(8,128)S(1)}, f32[96,2304]{1,0:T(8,128)S(1)}, f32[8,2,1152]{2,1,0:T(2,128)S(1)}, f32[8,2,96]{2,1,0:T(2,128)S(1)}) custom-call(bf16[2,256,768]{2,1,0:T(8,128)(2,1)S(1)} %get-tuple-element.56.attn_ref, bf16[2,256,768]{2,1,0:T(8,128)(2,1)S(1)} %get-tuple-element.55.ffn_ref, ...), custom_call_target="tpu_custom_call" | custom-call | tf_op jit(solution)/shard_map/pallas_call | solution.py:108
  203.7 1.1 multiply_reduce_fusion.4
  205.7 1.0 convolution_bitcast_fusion
  207.4 2.2 %multiply_add_fusion.2 = (f32[2,64,768]{2,1,0:T(8,128)}, bf16[2,64,768]{2,1,0:T(8,128)(2,1)}) fusion(f32[2,256,768]{2,1,0:T(8,128)} %copy-done.6, s32[]{:T(128)S(6)} %select_n.10, f32[2,256,768]{2,1,0:T(8,128)} %get-tuple-element.63, f32[2,64,768]{2,1,0:T(8,128)S(1)} %get-tuple-element.21, f32[2,64]{1,0:T(2,128)S(1)} %broadcast_multiply_fusion.4, ...), kind=kLoop, calls=%fused_computation.76 | loop fusion | flops 884736 | bytes 2569732 | tf_op jit(solution)/shard_map/add | solution.py:470
  (76 shorter events, 12.9 us)
Async XLA Ops:
  7.2 4.6 %copy-start = (bf16[96,1152]{1,0:T(8,128)(2,1)S(1)}, bf16[96,1152]{1,0:T(8,128)(2,1)}, u32[]{:S(2)}) copy-start(bf16[96,1152]{1,0:T(8,128)(2,1)} %w_ref.3) | copy-start | bytes 663556
  7.2 4.6 %copy-start.3 = (bf16[2,64,768]{2,1,0:T(8,128)(2,1)S(1)}, bf16[2,64,768]{2,1,0:T(8,128)(2,1)}, u32[]{:S(2)}) copy-start(bf16[2,64,768]{2,1,0:T(8,128)(2,1)} %x_ref.1) | copy-start | bytes 589828
  7.2 92.9 %all-gather.2.cloned.1.call-start = ((), (), s32[]{:S(2)}) async-start(), calls=%async_computation | async-start | bytes 2654208 | tf_op jit(solution)/shard_map/all_gather | solution.py:58
  37.4 5.1 %copy-start.1 = (bf16[8,96,768]{2,1,0:T(8,128)(2,1)}, bf16[8,96,768]{2,1,0:T(8,128)(2,1)S(1)}, u32[]{:S(2)}) copy-start(bf16[8,96,768]{2,1,0:T(8,128)(2,1)S(1)} %get-tuple-element.19) | copy-start | bytes 3538948
  38.9 3.6 %copy-start.10 = (bf16[2,256,576]{1,2,0:T(8,128)(2,1)}, bf16[2,256,576]{1,2,0:T(8,128)(2,1)S(1)}, u32[]{:S(2)}) copy-start(bf16[2,256,576]{1,2,0:T(8,128)(2,1)S(1)} %convolution_convert_fusion.2) | copy-start | bytes 1769476
  42.4 34.4 %copy-start.8 = (bf16[2,3,64,256]{3,2,1,0:T(8,128)(2,1)}, bf16[2,3,64,256]{3,2,1,0:T(8,128)(2,1)S(1)}, u32[]{:S(2)}) copy-start(bf16[2,3,64,256]{3,2,1,0:T(8,128)(2,1)S(1)} %convolution_convert_fusion.5) | copy-start | bytes 589828
  76.9 1.2 copy-start.4
  76.9 1.5 copy-start.12
  102.7 1.7 copy-start.14
  106.9 29.4 %copy-start.5 = (f32[2,256,768]{2,1,0:T(8,128)S(1)}, f32[2,256,768]{2,1,0:T(8,128)}, u32[]{:S(2)}) copy-start(f32[2,256,768]{2,1,0:T(8,128)} %copy-done.4) | copy-start | bytes 4718596
  137.1 1.6 copy-start.9
  138.7 2.4 %copy-start.6 = (f32[2,256,768]{2,1,0:T(8,128)}, f32[2,256,768]{2,1,0:T(8,128)S(1)}, u32[]{:S(2)}) copy-start(f32[2,256,768]{2,1,0:T(8,128)S(1)} %get-tuple-element.65) | copy-start | bytes 4718596
  138.7 1.8 copy-start.2
  141.1 1.4 copy-start.7
  142.5 1.1 copy-start.11
  202.0 1.1 copy-start.13
Sparse Core Ops, SparseCore 0:
  10.5 36.2 all-gather.1

commit v4 on v3

--- a/solution.py
+++ b/solution.py
@@ -52,10 +52,6 @@
 
 def gather_tensor(block, axis):
     return lax.all_gather(block, "tensor", axis=axis, tiled=True)
-
-
-def gather_weights(shard):
-    return lax.all_gather(shard, "dp", axis=0, tiled=True)
 
 
 def greet(axes):
@@ -214,18 +210,93 @@
     return ref.at[:, pl.ds(pl.multiple_of(at * size, size), size)]
 
 
-def reduce_kernel(part_ref, out_ref, recv, s0, s1):
+def finish_reduce(part_ref, out_ref, recv, first, sems):
     group = lax.axis_size("tensor")
     mine = lax.axis_index("tensor")
     size = part_ref.shape[1] // group
-    greet(("tensor",))
-    exchange("tensor", lambda peer: token_block(part_ref, peer, size), recv.at[mine], s0)
+    wait_all(first)
     total = token_block(part_ref, mine, size)[...].astype(f32)
     for step in range(1, group):
         total += recv[lax.rem(mine + step, group)].astype(f32)
     own = token_block(out_ref, mine, size)
     own[...] = total.astype(bf16)
-    exchange("tensor", lambda peer: own, own, s1)
+    return start_exchange("tensor", lambda peer: own, own, sems)
+
+
+def start_reduce(part_ref, recv, sems):
+    group = lax.axis_size("tensor")
+    size = part_ref.shape[1] // group
+    return start_exchange(
+        "tensor",
+        lambda peer: token_block(part_ref, peer, size),
+        recv.at[lax.axis_index("tensor")],
+        sems,
+    )
+
+
+def reduce_kernel(part_ref, out_ref, recv, s0, s1):
+    greet(("tensor",))
+    first = start_reduce(part_ref, recv, s0)
+    wait_all(finish_reduce(part_ref, out_ref, recv, first, s1))
+
+
+def reduce_gather_kernel(part_ref, shard_ref, out_ref, w_all, recv, s0, s1, s2, s3):
+    count = lax.axis_size("dp")
+    me = lax.axis_index("dp")
+    pairs = count // 2
+    chip, side = me // 2, lax.rem(me, 2)
+    sibling = 2 * chip + 1 - side
+    greet(("dp", "tensor"))
+
+    def send(source, at, to, sems, number):
+        copy = pltpu.make_async_remote_copy(
+            src_ref=source,
+            dst_ref=w_all.at[at],
+            send_sem=sems.at[0, number],
+            recv_sem=sems.at[1, number],
+            device_id={"dp": to},
+            device_id_type=MESH,
+        )
+        copy.start()
+        return copy
+
+    first = start_reduce(part_ref, recv, s0)
+    far = [
+        send(shard_ref, me, 2 * lax.rem(chip + step, pairs) + side, s2, step)
+        for step in range(1, pairs)
+    ]
+    near = [send(shard_ref, me, sibling, s3, 0)]
+    w_all[me] = shard_ref[...]
+    last = finish_reduce(part_ref, out_ref, recv, first, s1)
+    for step in range(1, pairs):
+        far[step - 1].wait()
+        came = 2 * lax.rem(chip + pairs - step, pairs) + side
+        near.append(send(w_all.at[came], came, sibling, s3, step))
+    wait_all(near)
+    wait_all(last)
+
+
+def reduce_and_gather(part, shard, number):
+    group, count = lax.axis_size("tensor"), lax.axis_size("dp")
+    rows, seq, width = part.shape
+    total, weights = call(
+        reduce_gather_kernel,
+        (
+            jax.ShapeDtypeStruct(part.shape, bf16),
+            jax.ShapeDtypeStruct((count,) + shard.shape, bf16),
+        ),
+        [
+            pltpu.VMEM((group, rows, seq // group, width), bf16),
+            sem_pair("tensor"),
+            sem_pair("tensor"),
+            pltpu.SemaphoreType.DMA((2, count // 2)),
+            pltpu.SemaphoreType.DMA((2, count // 2)),
+        ],
+        number,
+        part.astype(bf16),
+        shard,
+    )
+    return total.astype(f32), weights.reshape(count * shard.shape[0], shard.shape[1])
 
 
 def reduce_tensor(part, number):
@@ -397,10 +468,6 @@
     w_in = attn_weights[:, : 3 * local]
     proj_t = attn_weights[:, 3 * local :]
     cotangent = gather_tensor(out_grad, 1).astype(f32)
-    ffn_weights = gather_weights(ffn_shard)
-    up = ffn_weights[:, :units]
-    down_t = ffn_weights[:, units:]
-
     tokens = tokens.astype(f32)
     seq = tokens.shape[1]
 
@@ -414,7 +481,9 @@
     probs = shifted / jnp.sum(shifted, axis=-1, keepdims=True)
     probs_low = probs.astype(bf16)
     mixed = dot("lhqk,lkhe->lqhe", probs_low, values).reshape(rows, seq, local).astype(bf16)
-    attn_out = reduce_tensor(dot("lsd,ed->lse", mixed, proj_t), 3)
+    attn_out, ffn_weights = reduce_and_gather(dot("lsd,ed->lse", mixed, proj_t), ffn_shard, 3)
+    up = ffn_weights[:, :units]
+    down_t = ffn_weights[:, units:]
     resid = tokens + gate_a * attn_out
     normed_f, inverse_f = norm_parts(resid)
     ffn_in = (normed_f * (1.0 + scale_f) + shift_f).astype(bf16)

time: 217 us -> 208 us (0.959)
  between operations: 14.5 us -> 1.02 us
  Pallas kernels: 135 us -> 140 us
    pallas_call x4, Pallas kernels: 135 us -> 140 us  [call(): pl.pallas_call(kernel, out_shape=outs, in_specs=[VMEM] * len(args), out_s...]
    unnamed x34 -> x36, local copies, waits for them, and re-layouts: 6.02 us -> 3.69 us
  transfers between devices with their start and end apart: 1 -> 0, of which waited for: 0 -> 0; matrix products, arithmetic and copies ran while one was open for 4% -> 0% of each run, Pallas kernels for 27% -> 0%
where the time goes in v4:
time: 208 us; the launch traced here: 207 us
  Pallas kernels  140 us (67%)
  blocking collectives  21.8 us (10%)
  matrix products  19.6 us (9%)
  local copies, waits for them, and re-layouts  12.9 us (6%)
  other arithmetic  11.6 us (6%)
    pallas_call x4, Pallas kernels, call(): pl.pallas_call(kernel, out_shape=outs, in_specs=[VMEM] * len(args), out_s...  140 us
    all_gather x1, blocking collectives, gather_tensor(): return lax.all_gather(block, 'tensor', axis=axis, tiled=True)  21.8 us
    dot_general x18, matrix products, dot(): return jnp.einsum(form, left, right, preferred_element_type=f32)  17.8 us
    concatenate x1, local copies, waits for them, and re-layouts, shards(): jnp.concatenate([dot('lsd,lse->de', attn_in, d_projected).astype(bf16), d...  5.81 us

profile of v4, /device:TPU:0, one launch (start us, length us, event | category | flops | bytes accessed | tf_op | source)
XLA Modules:
  0.0 207.4 jit_solution(14229992620615178612)
XLA Ops:
  1.5 0.9 copy.33
  2.4 0.9 slice_bitcast_fusion.32
  3.4 1.0 pad_maximum_fusion.2.shard_ref
  4.4 21.8 %all_gather.3 = bf16[2,256,768]{2,1,0:T(8,128)(2,1)} all-gather(bf16[2,64,768]{2,1,0:T(8,128)(2,1)} %param.15), channel_id=1, replica_groups=mesh['dp'=8,'tensor'=4] {'tensor'}, dimensions={1}, use_global_device_ids=true | all-gather | bytes 983040 | tf_op jit(solution)/shard_map/all_gather | solution.py:54
  26.2 22.4 %shard_map.143 = (f32[4,2,1152]{2,1,0:T(2,128)S(1)}, f32[8,2,96]{2,1,0:T(2,128)S(1)}, bf16[2,256,768]{2,1,0:T(8,128)(2,1)S(1)}, bf16[8,96,768]{2,1,0:T(8,128)(2,1)S(1)}) custom-call(f32[8,2,96]{2,1,0:T(2,128)S(1)} %bitcast.145, bf16[96,1152]{1,0:T(8,128)(2,1)S(1)} %copy-done, bf16[2,64,768]{2,1,0:T(8,128)(2,1)S(1)} %copy-done.3, ...), custom_call_target="tpu_custom_call" | custom-call | tf_op jit(solution)/shard_map/pallas_call | solution.py:104
  50.4 0.9 convolution_convert_fusion.2
  51.3 1.8 fusion.44
  53.1 1.7 convolution_convert_fusion.5
  55.4 34.1 %shard_map.144 = (bf16[2,256,768]{2,1,0:T(8,128)(2,1)S(1)}, bf16[8,96,1536]{2,1,0:T(8,128)(2,1)S(1)}) custom-call(bf16[2,256,768]{2,1,0:T(8,128)(2,1)S(1)} %convolution_convert_fusion.1.part_ref, bf16[96,1536]{1,0:T(8,128)(2,1)S(1)} %pad_maximum_fusion.2.shard_ref), custom_call_target="tpu_custom_call" | custom-call | tf_op jit(solution)/shard_map/pallas_call | solution.py:104
  90.1 0.9 fusion.28
  91.5 1.7 fusion.15
  94.0 35.9 %shard_map.145 = bf16[2,256,768]{2,1,0:T(8,128)(2,1)S(1)} custom-call(bf16[2,256,768]{2,1,0:T(8,128)(2,1)S(1)} %convolution_convert_fusion.part_ref), custom_call_target="tpu_custom_call" | custom-call | tf_op jit(solution)/shard_map/pallas_call | solution.py:104
  130.7 2.1 %fusion.17 = (f32[2,768]{1,0:T(2,128)}, bf16[2,256,768]{2,1,0:T(8,128)(2,1)S(1)}, f32[2,768]{1,0:T(2,128)}, f32[2,256,768]{2,1,0:T(8,128)S(1)}) fusion(bf16[2,256,768]{2,1,0:T(8,128)(2,1)S(1)} %copy-done.7, bf16[2,256,768]{2,1,0:T(8,128)(2,1)S(1)} %get-tuple-element.22, f32[2,256]{1,0:T(2,128)S(1)} %broadcast_multiply_fusion, ...), kind=kOutput, calls=%fused_computation.37 | convolution fusion | flops 613807104 | bytes 9070592 | tf_op jit(solution)/shard_map/lsn,en->lse/dot_general | solution.py:50
  132.8 1.1 bitcast_convert_fusion
  136.3 1.1 bitcast_convert_fusion.1
  140.2 2.8 %multiply_reduce_fusion = (f32[2,768]{1,0:T(2,128)S(1)}, f32[2,768]{1,0:T(2,128)S(1)}, bf16[2,256,768]{2,1,0:T(8,128)(2,1)S(1)}, f32[2,256,768]{2,1,0:T(8,128)}) fusion(f32[2,256]{1,0:T(2,128)} %copy-done.15, f32[2,256]{1,0:T(2,128)S(1)} %broadcast_multiply_fusion.3, bf16[2,256,768]{2,1,0:T(8,128)(2,1)S(1)} %get-tuple-element.19, ...), kind=kOutput, calls=%fused_computation.41 | convolution fusion | flops 455734272 | bytes 4734976 | tf_op jit(solution)/shard_map/lse,de->lsd/dot_general | solution.py:50
  143.0 2.1 pad_maximum_fusion
  145.1 5.8 %copy.46 = bf16[768,2304]{1,0:T(8,128)(2,1)} copy(bf16[768,2304]{0,1:T(8,128)(2,1)} %pad_maximum_fusion) | data formatting | bytes 7077888 | tf_op jit(solution)/shard_map/concatenate | solution.py:516
  151.0 48.1 %shard_map.146 = (f32[2,64,768]{2,1,0:T(8,128)S(1)}, f32[2,64,768]{2,1,0:T(8,128)S(1)}, f32[96,2304]{1,0:T(8,128)S(1)}, f32[8,2,1152]{2,1,0:T(2,128)S(1)}, f32[8,2,96]{2,1,0:T(2,128)S(1)}) custom-call(bf16[2,256,768]{2,1,0:T(8,128)(2,1)S(1)} %get-tuple-element.60.attn_ref, bf16[2,256,768]{2,1,0:T(8,128)(2,1)S(1)} %get-tuple-element.59.ffn_ref, ...), custom_call_target="tpu_custom_call" | custom-call | tf_op jit(solution)/shard_map/pallas_call | solution.py:104
  199.2 1.3 negate_add_fusion
  200.5 1.1 multiply_reduce_fusion.4
  201.6 2.2 %multiply_add_fusion.2 = (f32[2,64,768]{2,1,0:T(8,128)}, bf16[2,64,768]{2,1,0:T(8,128)(2,1)}) fusion(f32[2,256,768]{2,1,0:T(8,128)} %copy-done.5, s32[]{:T(128)S(6)} %select_n.10, f32[2,256,768]{2,1,0:T(8,128)} %get-tuple-element.67, f32[2,64,768]{2,1,0:T(8,128)S(1)} %get-tuple-element.25, f32[2,64]{1,0:T(2,128)S(1)} %broadcast_multiply_fusion.4, ...), kind=kLoop, calls=%fused_computation.76 | loop fusion | flops 884736 | bytes 2569732 | tf_op jit(solution)/shard_map/add | solution.py:539
  204.0 0.9 slice_bitcast_fusion.12
  206.3 1.0 convolution_bitcast_fusion
  (75 shorter events, 12.9 us)
Async XLA Ops:
  0.6 25.5 %copy-start = (bf16[96,1152]{1,0:T(8,128)(2,1)S(1)}, bf16[96,1152]{1,0:T(8,128)(2,1)}, u32[]{:S(2)}) copy-start(bf16[96,1152]{1,0:T(8,128)(2,1)} %w_ref.3) | copy-start | bytes 663556
  0.6 25.5 %copy-start.3 = (bf16[2,64,768]{2,1,0:T(8,128)(2,1)S(1)}, bf16[2,64,768]{2,1,0:T(8,128)(2,1)}, u32[]{:S(2)}) copy-start(bf16[2,64,768]{2,1,0:T(8,128)(2,1)} %x_ref.1) | copy-start | bytes 589828
  48.6 85.6 %copy-start.1 = (bf16[8,96,768]{2,1,0:T(8,128)(2,1)}, bf16[8,96,768]{2,1,0:T(8,128)(2,1)S(1)}, u32[]{:S(2)}) copy-start(bf16[8,96,768]{2,1,0:T(8,128)(2,1)S(1)} %get-tuple-element.21) | copy-start | bytes 3538948
  48.6 41.5 %copy-start.11 = (f32[2,768]{1,0:T(2,128)}, f32[2,768]{1,0:T(2,128)S(1)}, u32[]{:S(2)}) copy-start(f32[2,768]{1,0:T(2,128)S(1)} %get-tuple-element.74) | copy-start | bytes 18436
  49.2 89.8 %copy-start.15 = (f32[2,256]{1,0:T(2,128)}, f32[2,256]{1,0:T(2,128)S(1)}, u32[]{:S(2)}) copy-start(f32[2,256]{1,0:T(2,128)S(1)} %add_rsqrt_fusion.1) | copy-start | bytes 6148
  51.3 3.5 %copy-start.8 = (bf16[2,256,576]{1,2,0:T(8,128)(2,1)}, bf16[2,256,576]{1,2,0:T(8,128)(2,1)S(1)}, u32[]{:S(2)}) copy-start(bf16[2,256,576]{1,2,0:T(8,128)(2,1)S(1)} %convolution_convert_fusion.2) | copy-start | bytes 1769476
  89.8 46.2 %copy-start.4 = (f32[2,256,768]{2,1,0:T(8,128)}, f32[2,256,768]{2,1,0:T(8,128)S(1)}, u32[]{:S(2)}) copy-start(f32[2,256,768]{2,1,0:T(8,128)S(1)} %get-tuple-element.57) | copy-start | bytes 4718596
  90.1 1.4 copy-start.7
  132.8 2.0 copy-start.5
  134.2 1.4 copy-start.6
  135.6 0.7 copy-start.12
  136.3 1.2 copy-start.9
  138.9 1.3 copy-start.2
  145.1 5.8 %copy-start.14 = (f32[2,768]{1,0:T(2,128)S(1)}, f32[2,768]{1,0:T(2,128)}, u32[]{:S(2)}) copy-start(f32[2,768]{1,0:T(2,128)} %get-tuple-element.68) | copy-start | bytes 18436
  145.1 5.9 %copy-start.13 = (f32[2,768]{1,0:T(2,128)S(1)}, f32[2,768]{1,0:T(2,128)}, u32[]{:S(2)}) copy-start(f32[2,768]{1,0:T(2,128)} %get-tuple-element.58) | copy-start | bytes 18436
  203.9 2.5 %copy-start.10 = (bf16[8,2,96]{2,1,0:T(2,128)(2,1)S(1)}, bf16[8,2,96]{2,1,0:T(2,128)(2,1)}, u32[]{:S(2)}) copy-start(bf16[8,2,96]{2,1,0:T(2,128)(2,1)} %convert_element_type.122) | copy-start | bytes 9220
